TPU v7x, 256 devices: a whole 4x4x8 slice. The times are simulated.
256 devices in a mesh: tm: 8 (over y, core), space: 32 (over z, x).
Axes of the slice: x: 4, y: 4, z: 8, core: 2. Of those that a mesh axis runs over, the one named last changes fastest.
Arguments:
- node_states: float32 [8, 9, 131072], P('tm', None, 'space'), may hold values from -6 to 6
- strengths: float32 [3, 131072], P(None, 'space'), may hold values from -4 to 4
- start_state: float32 [3, 131072], P(None, 'space'), may hold values from -6 to 6
- lists: int32 [1024, 12], replicated, may hold values from 0 to 1023, as said below
- counts: int32 [32], replicated, may hold values from 16 to 32, as said below
Outputs:
- new_nodes: float32 [8, 9, 131072], P('tm', None, 'space')
Inputs may be any that keep to these rules, and one draw needn't show every extreme that they name: `lists`: every entry names a live block; the entries of one row are distinct; over all rows of one shard, live or not, each other shard has between 1 and 2 distinct blocks named, and some pair of shards reaches 2; a shard's own blocks may be named freely. `counts`: number of live blocks of each shard; slots from that number to 31 hold no particles that matter.
All inputs are finite; a program needn't handle non-finite values.
Results may differ from a plain program's by a relative error of at most 0.00005.
Values sent between devices are 32-bit elements; how exact they have to be, the bound alone decides.
No kernel may reach another device: no remote copies, remote signals or barrier semaphores. Data moves between devices by JAX's collectives and lax.ppermute only.
A program may use at most 64 MiB of HBM per device.

v0:
```python
import math

import jax
import jax.numpy as jnp
import numpy as np
from jax import lax
from jax.sharding import PartitionSpec as P

core_sq = 0.25
step_size = 1.0
group_size = 2


def entering(value, axis, join, neutral):
    count, mine = (lax.axis_size(axis), lax.axis_index(axis))
    pieces = lax.all_gather(value, axis)
    subtotal = jnp.full_like(value, 0) + jnp.asarray(neutral, value.dtype)

    def step(position, subtotal):
        longer = join(subtotal, pieces[position])
        return jnp.where(position < mine, longer, subtotal)

    return lax.fori_loop(0, count - 1, step, subtotal)


def radau_matrix():
    sqrt_six = math.sqrt(6.0)
    return np.array(
        [
            [
                (88.0 - 7.0 * sqrt_six) / 360.0,
                (296.0 - 169.0 * sqrt_six) / 1800.0,
                (-2.0 + 3.0 * sqrt_six) / 225.0,
            ],
            [
                (296.0 + 169.0 * sqrt_six) / 1800.0,
                (88.0 + 7.0 * sqrt_six) / 360.0,
                (-2.0 - 3.0 * sqrt_six) / 225.0,
            ],
            [(16.0 - sqrt_six) / 36.0, (16.0 + sqrt_six) / 36.0, 1.0 / 9.0],
        ]
    )


def cross_rows(former, latter):
    return jnp.stack(
        [
            former[:, 1] * latter[:, 2] - former[:, 2] * latter[:, 1],
            former[:, 2] * latter[:, 0] - former[:, 0] * latter[:, 2],
            former[:, 0] * latter[:, 1] - former[:, 1] * latter[:, 0],
        ],
        axis=1,
    )


def block_velocity(targets, sources):
    listed = jnp.transpose(sources, (1, 0, 2)).reshape(12, -1)
    places = listed[:9].reshape(3, 3, -1)
    strength = jnp.broadcast_to(listed[9:][None], places.shape)
    target_pos = targets.reshape(3, 3, -1)
    offset = target_pos[:, :, None, :] - places[:, :, :, None]
    kernel = (jnp.sum(offset * offset, axis=1) + core_sq) ** (-1.5)
    weights = jnp.concatenate([strength, cross_rows(places, strength)], axis=1)
    totals = jnp.einsum("mks,msb->mkb", weights, kernel, precision=lax.Precision.HIGHEST)
    spread = cross_rows(target_pos, totals[:, :3]) - totals[:, 3:]
    return (spread * (-0.25 / math.pi)).reshape(9, -1)


def shards(node_states, strengths, start_state, lists, counts):
    groups = lax.axis_size("space")
    rank_space = lax.axis_index("space")
    blocks_dev = lists.shape[0] // groups
    block_size = node_states.shape[2] // blocks_dev
    list_len = lists.shape[1]
    payload = jnp.concatenate([node_states[0], strengths], axis=0)
    own_blocks = payload.reshape(12, blocks_dev, block_size).transpose(1, 0, 2)
    my_lists = lax.dynamic_slice_in_dim(lists, rank_space * blocks_dev, blocks_dev, 0)
    source_table = lax.all_gather(own_blocks, "space", axis=0, tiled=True)
    targets_all = node_states[0].reshape(9, blocks_dev, block_size).transpose(1, 0, 2)
    live_count = lax.dynamic_index_in_dim(counts, rank_space, 0, keepdims=False)

    def one_group(packed):
        group_slots, group_targets = packed
        group_sources = jnp.take(source_table, group_slots.reshape(-1), axis=0)
        group_sources = group_sources.reshape(
            group_slots.shape[0], group_slots.shape[1], 12, block_size
        )
        return jax.vmap(block_velocity)(group_targets, group_sources)

    steps_count = blocks_dev // group_size
    velocity = lax.map(
        one_group,
        (
            my_lists.reshape(steps_count, group_size, list_len),
            targets_all.reshape(steps_count, group_size, 9, block_size),
        ),
    )
    velocity = velocity.reshape(blocks_dev, 9, block_size)
    live_rows = jnp.arange(blocks_dev, dtype=jnp.int32) < live_count
    velocity = jnp.where(live_rows[:, None, None], velocity, jnp.zeros_like(velocity))
    rates = velocity.transpose(1, 0, 2).reshape(3, 3, blocks_dev * block_size)
    table = jnp.asarray(radau_matrix(), jnp.float32)
    quadrature = step_size * jnp.einsum(
        "mj,jcp->mcp", table, rates, precision=lax.Precision.HIGHEST
    )
    increment = quadrature[2]
    carried = entering(
        increment, "tm", lambda earlier, coming: earlier + coming, jnp.zeros_like(increment)
    )
    updated = start_state + carried + quadrature
    return updated.reshape(1, 9, -1)


def solution(mesh):
    return jax.shard_map(
        shards,
        mesh=mesh,
        in_specs=(P("tm", None, "space"), P(None, "space"), P(None, "space"), P(), P()),
        out_specs=P("tm", None, "space"),
        check_vma=False,
    )
```

profile of v0, /device:TPU:1, one launch (start us, length us, event | category | flops | bytes accessed | tf_op | source)
XLA Modules:
  0.0 363.8 jit_solution(13587070261722279353)
XLA Ops:
  6.5 0.9 copy.97
  7.4 1.6 maximum_bitcast_fusion
  9.2 1.3 dynamic_slice.22
  11.1 90.9 %all-gather.2.cloned.1.call-done = f32[1024,12,128]{2,0,1:T(8,128)} async-done(((f32[32,12,128]{2,0,1:T(8,128)}), f32[1024,12,128]{2,0,1:T(8,128)}) %all-gather.2.cloned.1.call-update) | async-done | bytes 6291472 | tf_op jit(solution)/shard_map/all_gather | solution.py:78
  102.1 9.8 %copy.81 = f32[1024,12,128]{2,1,0:T(8,128)} copy(f32[1024,12,128]{2,0,1:T(8,128)} %all-gather.2.cloned.1.call-done) | data formatting | bytes 12582912 | tf_op jit(solution)/shard_map/while | solution.py:91
  111.9 228.4 %while.24 = (s32[]{:T(128)}, f32[16,2,9,128]{3,1,0,2:T(2,128)S(1)}, f32[16,2,9,128]{3,1,0,2:T(2,128)}, s32[16,2,12]{2,1,0:T(2,128)S(1)}, f32[1024,12,128]{2,1,0:T(8,128)}, /*index=5*/s32[]{:T(128)}) while((s32[]{:T(128)}, f32[16,2,9,128]{3,1,0,2:T(2,128)S(1)}, f32[16,2,9,128]{3,1,0,2:T(2,128)}, s32[16,2,12]{2,1,0:T(2,128)S(1)}, ...), condition=%wide.region_2.3_spmd, body=%wide.region_0.2_spmd.sunk | while | flops 95854552 | bytes 11884417 | solution.py:91
  112.0 3.9 %gather_fusion = f32[24,12,128]{2,1,0:T(8,128)S(1)} fusion(f32[1024,12,128]{2,1,0:T(8,128)} %get-tuple-element.283, s32[1024]{0:T(1024)S(1)} %pad_clamp_fusion.2), kind=kCustom, calls=%fused_computation.clone.1 | custom fusion | bytes 295008 | tf_op jit(solution)/shard_map/while/body/eval_jaxpr/jit(_take)/gather | solution.py:84
  116.3 0.7 constant_dynamic-slice_fusion.5
  117.0 4.7 %multiply_reduce_fusion.2 = f32[2,3,1536,128]{3,2,1,0:T(8,128)S(1)} fusion(f32[2,3,3,1536]{3,2,1,0:T(4,128)S(1)} %copy.104, f32[2,3,3,128]{3,2,1,0:T(4,128)S(1)} %copy.105), kind=kLoop, calls=%fused_computation.1.clone.1 | loop fusion | flops 9437184 | bytes 4838400 | tf_op jit(solution)/shard_map/while/body/eval_jaxpr/vmap()/reduce_sum | solution.py:62
  121.8 4.2 %fusion.31 = f32[2,3,6,128]{3,2,1,0:T(8,128)S(1)} fusion(f32[2,3,1536,128]{3,2,1,0:T(8,128)S(1)} %multiply_reduce_fusion.2, f32[2,3,1,1536]{3,2,1,0:T(1,128)S(1)} %get-tuple-element.257, f32[2,3,1,1536]{3,2,1,0:T(1,128)S(1)} %get-tuple-element.258, f32[2,3,1,1536]{3,2,1,0:T(1,128)S(1)} %get-tuple-element.259, f32[2,3,3,1536]{3,2,1,0:T(4,128)S(1)} %broadcast_in_dim.68), kind=kOutput, calls=%fused_computation.2.clone.1 | convolution fusion | flops 86280192 | bytes 4958208 | tf_op jit(solution)/shard_map/while/body/eval_jaxpr/vmap(mks,msb->mkb)/dot_general | solution.py:64
  126.2 3.9 %gather_fusion = f32[24,12,128]{2,1,0:T(8,128)S(1)} fusion(f32[1024,12,128]{2,1,0:T(8,128)} %get-tuple-element.283, s32[1024]{0:T(1024)S(1)} %pad_clamp_fusion.2), kind=kCustom, calls=%fused_computation.clone.1 | custom fusion | bytes 295008 | tf_op jit(solution)/shard_map/while/body/eval_jaxpr/jit(_take)/gather | solution.py:84
  131.3 4.7 %multiply_reduce_fusion.2 = f32[2,3,1536,128]{3,2,1,0:T(8,128)S(1)} fusion(f32[2,3,3,1536]{3,2,1,0:T(4,128)S(1)} %copy.104, f32[2,3,3,128]{3,2,1,0:T(4,128)S(1)} %copy.105), kind=kLoop, calls=%fused_computation.1.clone.1 | loop fusion | flops 9437184 | bytes 4838400 | tf_op jit(solution)/shard_map/while/body/eval_jaxpr/vmap()/reduce_sum | solution.py:62
  136.1 4.2 %fusion.31 = f32[2,3,6,128]{3,2,1,0:T(8,128)S(1)} fusion(f32[2,3,1536,128]{3,2,1,0:T(8,128)S(1)} %multiply_reduce_fusion.2, f32[2,3,1,1536]{3,2,1,0:T(1,128)S(1)} %get-tuple-element.257, f32[2,3,1,1536]{3,2,1,0:T(1,128)S(1)} %get-tuple-element.258, f32[2,3,1,1536]{3,2,1,0:T(1,128)S(1)} %get-tuple-element.259, f32[2,3,3,1536]{3,2,1,0:T(4,128)S(1)} %broadcast_in_dim.68), kind=kOutput, calls=%fused_computation.2.clone.1 | convolution fusion | flops 86280192 | bytes 4958208 | tf_op jit(solution)/shard_map/while/body/eval_jaxpr/vmap(mks,msb->mkb)/dot_general | solution.py:64
  140.5 3.9 %gather_fusion = f32[24,12,128]{2,1,0:T(8,128)S(1)} fusion(f32[1024,12,128]{2,1,0:T(8,128)} %get-tuple-element.283, s32[1024]{0:T(1024)S(1)} %pad_clamp_fusion.2), kind=kCustom, calls=%fused_computation.clone.1 | custom fusion | bytes 295008 | tf_op jit(solution)/shard_map/while/body/eval_jaxpr/jit(_take)/gather | solution.py:84
  145.6 4.7 %multiply_reduce_fusion.2 = f32[2,3,1536,128]{3,2,1,0:T(8,128)S(1)} fusion(f32[2,3,3,1536]{3,2,1,0:T(4,128)S(1)} %copy.104, f32[2,3,3,128]{3,2,1,0:T(4,128)S(1)} %copy.105), kind=kLoop, calls=%fused_computation.1.clone.1 | loop fusion | flops 9437184 | bytes 4838400 | tf_op jit(solution)/shard_map/while/body/eval_jaxpr/vmap()/reduce_sum | solution.py:62
  150.3 4.2 %fusion.31 = f32[2,3,6,128]{3,2,1,0:T(8,128)S(1)} fusion(f32[2,3,1536,128]{3,2,1,0:T(8,128)S(1)} %multiply_reduce_fusion.2, f32[2,3,1,1536]{3,2,1,0:T(1,128)S(1)} %get-tuple-element.257, f32[2,3,1,1536]{3,2,1,0:T(1,128)S(1)} %get-tuple-element.258, f32[2,3,1,1536]{3,2,1,0:T(1,128)S(1)} %get-tuple-element.259, f32[2,3,3,1536]{3,2,1,0:T(4,128)S(1)} %broadcast_in_dim.68), kind=kOutput, calls=%fused_computation.2.clone.1 | convolution fusion | flops 86280192 | bytes 4958208 | tf_op jit(solution)/shard_map/while/body/eval_jaxpr/vmap(mks,msb->mkb)/dot_general | solution.py:64
  154.8 3.9 %gather_fusion = f32[24,12,128]{2,1,0:T(8,128)S(1)} fusion(f32[1024,12,128]{2,1,0:T(8,128)} %get-tuple-element.283, s32[1024]{0:T(1024)S(1)} %pad_clamp_fusion.2), kind=kCustom, calls=%fused_computation.clone.1 | custom fusion | bytes 295008 | tf_op jit(solution)/shard_map/while/body/eval_jaxpr/jit(_take)/gather | solution.py:84
  159.1 0.7 constant_dynamic-slice_fusion.5
  159.8 4.7 %multiply_reduce_fusion.2 = f32[2,3,1536,128]{3,2,1,0:T(8,128)S(1)} fusion(f32[2,3,3,1536]{3,2,1,0:T(4,128)S(1)} %copy.104, f32[2,3,3,128]{3,2,1,0:T(4,128)S(1)} %copy.105), kind=kLoop, calls=%fused_computation.1.clone.1 | loop fusion | flops 9437184 | bytes 4838400 | tf_op jit(solution)/shard_map/while/body/eval_jaxpr/vmap()/reduce_sum | solution.py:62
  164.6 4.2 %fusion.31 = f32[2,3,6,128]{3,2,1,0:T(8,128)S(1)} fusion(f32[2,3,1536,128]{3,2,1,0:T(8,128)S(1)} %multiply_reduce_fusion.2, f32[2,3,1,1536]{3,2,1,0:T(1,128)S(1)} %get-tuple-element.257, f32[2,3,1,1536]{3,2,1,0:T(1,128)S(1)} %get-tuple-element.258, f32[2,3,1,1536]{3,2,1,0:T(1,128)S(1)} %get-tuple-element.259, f32[2,3,3,1536]{3,2,1,0:T(4,128)S(1)} %broadcast_in_dim.68), kind=kOutput, calls=%fused_computation.2.clone.1 | convolution fusion | flops 86280192 | bytes 4958208 | tf_op jit(solution)/shard_map/while/body/eval_jaxpr/vmap(mks,msb->mkb)/dot_general | solution.py:64
  169.1 3.9 %gather_fusion = f32[24,12,128]{2,1,0:T(8,128)S(1)} fusion(f32[1024,12,128]{2,1,0:T(8,128)} %get-tuple-element.283, s32[1024]{0:T(1024)S(1)} %pad_clamp_fusion.2), kind=kCustom, calls=%fused_computation.clone.1 | custom fusion | bytes 295008 | tf_op jit(solution)/shard_map/while/body/eval_jaxpr/jit(_take)/gather | solution.py:84
  173.4 0.7 constant_dynamic-slice_fusion.5
  174.1 4.7 %multiply_reduce_fusion.2 = f32[2,3,1536,128]{3,2,1,0:T(8,128)S(1)} fusion(f32[2,3,3,1536]{3,2,1,0:T(4,128)S(1)} %copy.104, f32[2,3,3,128]{3,2,1,0:T(4,128)S(1)} %copy.105), kind=kLoop, calls=%fused_computation.1.clone.1 | loop fusion | flops 9437184 | bytes 4838400 | tf_op jit(solution)/shard_map/while/body/eval_jaxpr/vmap()/reduce_sum | solution.py:62
  178.9 4.2 %fusion.31 = f32[2,3,6,128]{3,2,1,0:T(8,128)S(1)} fusion(f32[2,3,1536,128]{3,2,1,0:T(8,128)S(1)} %multiply_reduce_fusion.2, f32[2,3,1,1536]{3,2,1,0:T(1,128)S(1)} %get-tuple-element.257, f32[2,3,1,1536]{3,2,1,0:T(1,128)S(1)} %get-tuple-element.258, f32[2,3,1,1536]{3,2,1,0:T(1,128)S(1)} %get-tuple-element.259, f32[2,3,3,1536]{3,2,1,0:T(4,128)S(1)} %broadcast_in_dim.68), kind=kOutput, calls=%fused_computation.2.clone.1 | convolution fusion | flops 86280192 | bytes 4958208 | tf_op jit(solution)/shard_map/while/body/eval_jaxpr/vmap(mks,msb->mkb)/dot_general | solution.py:64
  183.3 3.9 %gather_fusion = f32[24,12,128]{2,1,0:T(8,128)S(1)} fusion(f32[1024,12,128]{2,1,0:T(8,128)} %get-tuple-element.283, s32[1024]{0:T(1024)S(1)} %pad_clamp_fusion.2), kind=kCustom, calls=%fused_computation.clone.1 | custom fusion | bytes 295008 | tf_op jit(solution)/shard_map/while/body/eval_jaxpr/jit(_take)/gather | solution.py:84
  187.7 0.7 constant_dynamic-slice_fusion.5
  188.4 4.7 %multiply_reduce_fusion.2 = f32[2,3,1536,128]{3,2,1,0:T(8,128)S(1)} fusion(f32[2,3,3,1536]{3,2,1,0:T(4,128)S(1)} %copy.104, f32[2,3,3,128]{3,2,1,0:T(4,128)S(1)} %copy.105), kind=kLoop, calls=%fused_computation.1.clone.1 | loop fusion | flops 9437184 | bytes 4838400 | tf_op jit(solution)/shard_map/while/body/eval_jaxpr/vmap()/reduce_sum | solution.py:62
  193.2 4.2 %fusion.31 = f32[2,3,6,128]{3,2,1,0:T(8,128)S(1)} fusion(f32[2,3,1536,128]{3,2,1,0:T(8,128)S(1)} %multiply_reduce_fusion.2, f32[2,3,1,1536]{3,2,1,0:T(1,128)S(1)} %get-tuple-element.257, f32[2,3,1,1536]{3,2,1,0:T(1,128)S(1)} %get-tuple-element.258, f32[2,3,1,1536]{3,2,1,0:T(1,128)S(1)} %get-tuple-element.259, f32[2,3,3,1536]{3,2,1,0:T(4,128)S(1)} %broadcast_in_dim.68), kind=kOutput, calls=%fused_computation.2.clone.1 | convolution fusion | flops 86280192 | bytes 4958208 | tf_op jit(solution)/shard_map/while/body/eval_jaxpr/vmap(mks,msb->mkb)/dot_general | solution.py:64
  197.6 3.9 %gather_fusion = f32[24,12,128]{2,1,0:T(8,128)S(1)} fusion(f32[1024,12,128]{2,1,0:T(8,128)} %get-tuple-element.283, s32[1024]{0:T(1024)S(1)} %pad_clamp_fusion.2), kind=kCustom, calls=%fused_computation.clone.1 | custom fusion | bytes 295008 | tf_op jit(solution)/shard_map/while/body/eval_jaxpr/jit(_take)/gather | solution.py:84
  201.9 0.7 constant_dynamic-slice_fusion.5
  202.7 4.7 %multiply_reduce_fusion.2 = f32[2,3,1536,128]{3,2,1,0:T(8,128)S(1)} fusion(f32[2,3,3,1536]{3,2,1,0:T(4,128)S(1)} %copy.104, f32[2,3,3,128]{3,2,1,0:T(4,128)S(1)} %copy.105), kind=kLoop, calls=%fused_computation.1.clone.1 | loop fusion | flops 9437184 | bytes 4838400 | tf_op jit(solution)/shard_map/while/body/eval_jaxpr/vmap()/reduce_sum | solution.py:62
  207.5 4.2 %fusion.31 = f32[2,3,6,128]{3,2,1,0:T(8,128)S(1)} fusion(f32[2,3,1536,128]{3,2,1,0:T(8,128)S(1)} %multiply_reduce_fusion.2, f32[2,3,1,1536]{3,2,1,0:T(1,128)S(1)} %get-tuple-element.257, f32[2,3,1,1536]{3,2,1,0:T(1,128)S(1)} %get-tuple-element.258, f32[2,3,1,1536]{3,2,1,0:T(1,128)S(1)} %get-tuple-element.259, f32[2,3,3,1536]{3,2,1,0:T(4,128)S(1)} %broadcast_in_dim.68), kind=kOutput, calls=%fused_computation.2.clone.1 | convolution fusion | flops 86280192 | bytes 4958208 | tf_op jit(solution)/shard_map/while/body/eval_jaxpr/vmap(mks,msb->mkb)/dot_general | solution.py:64
  211.9 3.9 %gather_fusion = f32[24,12,128]{2,1,0:T(8,128)S(1)} fusion(f32[1024,12,128]{2,1,0:T(8,128)} %get-tuple-element.283, s32[1024]{0:T(1024)S(1)} %pad_clamp_fusion.2), kind=kCustom, calls=%fused_computation.clone.1 | custom fusion | bytes 295008 | tf_op jit(solution)/shard_map/while/body/eval_jaxpr/jit(_take)/gather | solution.py:84
  216.9 4.7 %multiply_reduce_fusion.2 = f32[2,3,1536,128]{3,2,1,0:T(8,128)S(1)} fusion(f32[2,3,3,1536]{3,2,1,0:T(4,128)S(1)} %copy.104, f32[2,3,3,128]{3,2,1,0:T(4,128)S(1)} %copy.105), kind=kLoop, calls=%fused_computation.1.clone.1 | loop fusion | flops 9437184 | bytes 4838400 | tf_op jit(solution)/shard_map/while/body/eval_jaxpr/vmap()/reduce_sum | solution.py:62
  221.7 4.2 %fusion.31 = f32[2,3,6,128]{3,2,1,0:T(8,128)S(1)} fusion(f32[2,3,1536,128]{3,2,1,0:T(8,128)S(1)} %multiply_reduce_fusion.2, f32[2,3,1,1536]{3,2,1,0:T(1,128)S(1)} %get-tuple-element.257, f32[2,3,1,1536]{3,2,1,0:T(1,128)S(1)} %get-tuple-element.258, f32[2,3,1,1536]{3,2,1,0:T(1,128)S(1)} %get-tuple-element.259, f32[2,3,3,1536]{3,2,1,0:T(4,128)S(1)} %broadcast_in_dim.68), kind=kOutput, calls=%fused_computation.2.clone.1 | convolution fusion | flops 86280192 | bytes 4958208 | tf_op jit(solution)/shard_map/while/body/eval_jaxpr/vmap(mks,msb->mkb)/dot_general | solution.py:64
  226.2 3.9 %gather_fusion = f32[24,12,128]{2,1,0:T(8,128)S(1)} fusion(f32[1024,12,128]{2,1,0:T(8,128)} %get-tuple-element.283, s32[1024]{0:T(1024)S(1)} %pad_clamp_fusion.2), kind=kCustom, calls=%fused_computation.clone.1 | custom fusion | bytes 295008 | tf_op jit(solution)/shard_map/while/body/eval_jaxpr/jit(_take)/gather | solution.py:84
  231.2 4.7 %multiply_reduce_fusion.2 = f32[2,3,1536,128]{3,2,1,0:T(8,128)S(1)} fusion(f32[2,3,3,1536]{3,2,1,0:T(4,128)S(1)} %copy.104, f32[2,3,3,128]{3,2,1,0:T(4,128)S(1)} %copy.105), kind=kLoop, calls=%fused_computation.1.clone.1 | loop fusion | flops 9437184 | bytes 4838400 | tf_op jit(solution)/shard_map/while/body/eval_jaxpr/vmap()/reduce_sum | solution.py:62
  236.0 4.2 %fusion.31 = f32[2,3,6,128]{3,2,1,0:T(8,128)S(1)} fusion(f32[2,3,1536,128]{3,2,1,0:T(8,128)S(1)} %multiply_reduce_fusion.2, f32[2,3,1,1536]{3,2,1,0:T(1,128)S(1)} %get-tuple-element.257, f32[2,3,1,1536]{3,2,1,0:T(1,128)S(1)} %get-tuple-element.258, f32[2,3,1,1536]{3,2,1,0:T(1,128)S(1)} %get-tuple-element.259, f32[2,3,3,1536]{3,2,1,0:T(4,128)S(1)} %broadcast_in_dim.68), kind=kOutput, calls=%fused_computation.2.clone.1 | convolution fusion | flops 86280192 | bytes 4958208 | tf_op jit(solution)/shard_map/while/body/eval_jaxpr/vmap(mks,msb->mkb)/dot_general | solution.py:64
  240.4 3.9 %gather_fusion = f32[24,12,128]{2,1,0:T(8,128)S(1)} fusion(f32[1024,12,128]{2,1,0:T(8,128)} %get-tuple-element.283, s32[1024]{0:T(1024)S(1)} %pad_clamp_fusion.2), kind=kCustom, calls=%fused_computation.clone.1 | custom fusion | bytes 295008 | tf_op jit(solution)/shard_map/while/body/eval_jaxpr/jit(_take)/gather | solution.py:84
  244.8 0.7 constant_dynamic-slice_fusion.5
  245.5 4.7 %multiply_reduce_fusion.2 = f32[2,3,1536,128]{3,2,1,0:T(8,128)S(1)} fusion(f32[2,3,3,1536]{3,2,1,0:T(4,128)S(1)} %copy.104, f32[2,3,3,128]{3,2,1,0:T(4,128)S(1)} %copy.105), kind=kLoop, calls=%fused_computation.1.clone.1 | loop fusion | flops 9437184 | bytes 4838400 | tf_op jit(solution)/shard_map/while/body/eval_jaxpr/vmap()/reduce_sum | solution.py:62
  250.3 4.2 %fusion.31 = f32[2,3,6,128]{3,2,1,0:T(8,128)S(1)} fusion(f32[2,3,1536,128]{3,2,1,0:T(8,128)S(1)} %multiply_reduce_fusion.2, f32[2,3,1,1536]{3,2,1,0:T(1,128)S(1)} %get-tuple-element.257, f32[2,3,1,1536]{3,2,1,0:T(1,128)S(1)} %get-tuple-element.258, f32[2,3,1,1536]{3,2,1,0:T(1,128)S(1)} %get-tuple-element.259, f32[2,3,3,1536]{3,2,1,0:T(4,128)S(1)} %broadcast_in_dim.68), kind=kOutput, calls=%fused_computation.2.clone.1 | convolution fusion | flops 86280192 | bytes 4958208 | tf_op jit(solution)/shard_map/while/body/eval_jaxpr/vmap(mks,msb->mkb)/dot_general | solution.py:64
  254.7 3.9 %gather_fusion = f32[24,12,128]{2,1,0:T(8,128)S(1)} fusion(f32[1024,12,128]{2,1,0:T(8,128)} %get-tuple-element.283, s32[1024]{0:T(1024)S(1)} %pad_clamp_fusion.2), kind=kCustom, calls=%fused_computation.clone.1 | custom fusion | bytes 295008 | tf_op jit(solution)/shard_map/while/body/eval_jaxpr/jit(_take)/gather | solution.py:84
  259.1 0.7 constant_dynamic-slice_fusion.5
  259.8 4.7 %multiply_reduce_fusion.2 = f32[2,3,1536,128]{3,2,1,0:T(8,128)S(1)} fusion(f32[2,3,3,1536]{3,2,1,0:T(4,128)S(1)} %copy.104, f32[2,3,3,128]{3,2,1,0:T(4,128)S(1)} %copy.105), kind=kLoop, calls=%fused_computation.1.clone.1 | loop fusion | flops 9437184 | bytes 4838400 | tf_op jit(solution)/shard_map/while/body/eval_jaxpr/vmap()/reduce_sum | solution.py:62
  264.6 4.2 %fusion.31 = f32[2,3,6,128]{3,2,1,0:T(8,128)S(1)} fusion(f32[2,3,1536,128]{3,2,1,0:T(8,128)S(1)} %multiply_reduce_fusion.2, f32[2,3,1,1536]{3,2,1,0:T(1,128)S(1)} %get-tuple-element.257, f32[2,3,1,1536]{3,2,1,0:T(1,128)S(1)} %get-tuple-element.258, f32[2,3,1,1536]{3,2,1,0:T(1,128)S(1)} %get-tuple-element.259, f32[2,3,3,1536]{3,2,1,0:T(4,128)S(1)} %broadcast_in_dim.68), kind=kOutput, calls=%fused_computation.2.clone.1 | convolution fusion | flops 86280192 | bytes 4958208 | tf_op jit(solution)/shard_map/while/body/eval_jaxpr/vmap(mks,msb->mkb)/dot_general | solution.py:64
  269.0 3.9 %gather_fusion = f32[24,12,128]{2,1,0:T(8,128)S(1)} fusion(f32[1024,12,128]{2,1,0:T(8,128)} %get-tuple-element.283, s32[1024]{0:T(1024)S(1)} %pad_clamp_fusion.2), kind=kCustom, calls=%fused_computation.clone.1 | custom fusion | bytes 295008 | tf_op jit(solution)/shard_map/while/body/eval_jaxpr/jit(_take)/gather | solution.py:84
  273.3 0.7 constant_dynamic-slice_fusion.5
  274.0 4.7 %multiply_reduce_fusion.2 = f32[2,3,1536,128]{3,2,1,0:T(8,128)S(1)} fusion(f32[2,3,3,1536]{3,2,1,0:T(4,128)S(1)} %copy.104, f32[2,3,3,128]{3,2,1,0:T(4,128)S(1)} %copy.105), kind=kLoop, calls=%fused_computation.1.clone.1 | loop fusion | flops 9437184 | bytes 4838400 | tf_op jit(solution)/shard_map/while/body/eval_jaxpr/vmap()/reduce_sum | solution.py:62
  278.8 4.2 %fusion.31 = f32[2,3,6,128]{3,2,1,0:T(8,128)S(1)} fusion(f32[2,3,1536,128]{3,2,1,0:T(8,128)S(1)} %multiply_reduce_fusion.2, f32[2,3,1,1536]{3,2,1,0:T(1,128)S(1)} %get-tuple-element.257, f32[2,3,1,1536]{3,2,1,0:T(1,128)S(1)} %get-tuple-element.258, f32[2,3,1,1536]{3,2,1,0:T(1,128)S(1)} %get-tuple-element.259, f32[2,3,3,1536]{3,2,1,0:T(4,128)S(1)} %broadcast_in_dim.68), kind=kOutput, calls=%fused_computation.2.clone.1 | convolution fusion | flops 86280192 | bytes 4958208 | tf_op jit(solution)/shard_map/while/body/eval_jaxpr/vmap(mks,msb->mkb)/dot_general | solution.py:64
  283.3 3.9 %gather_fusion = f32[24,12,128]{2,1,0:T(8,128)S(1)} fusion(f32[1024,12,128]{2,1,0:T(8,128)} %get-tuple-element.283, s32[1024]{0:T(1024)S(1)} %pad_clamp_fusion.2), kind=kCustom, calls=%fused_computation.clone.1 | custom fusion | bytes 295008 | tf_op jit(solution)/shard_map/while/body/eval_jaxpr/jit(_take)/gather | solution.py:84
  288.3 4.7 %multiply_reduce_fusion.2 = f32[2,3,1536,128]{3,2,1,0:T(8,128)S(1)} fusion(f32[2,3,3,1536]{3,2,1,0:T(4,128)S(1)} %copy.104, f32[2,3,3,128]{3,2,1,0:T(4,128)S(1)} %copy.105), kind=kLoop, calls=%fused_computation.1.clone.1 | loop fusion | flops 9437184 | bytes 4838400 | tf_op jit(solution)/shard_map/while/body/eval_jaxpr/vmap()/reduce_sum | solution.py:62
  293.1 4.2 %fusion.31 = f32[2,3,6,128]{3,2,1,0:T(8,128)S(1)} fusion(f32[2,3,1536,128]{3,2,1,0:T(8,128)S(1)} %multiply_reduce_fusion.2, f32[2,3,1,1536]{3,2,1,0:T(1,128)S(1)} %get-tuple-element.257, f32[2,3,1,1536]{3,2,1,0:T(1,128)S(1)} %get-tuple-element.258, f32[2,3,1,1536]{3,2,1,0:T(1,128)S(1)} %get-tuple-element.259, f32[2,3,3,1536]{3,2,1,0:T(4,128)S(1)} %broadcast_in_dim.68), kind=kOutput, calls=%fused_computation.2.clone.1 | convolution fusion | flops 86280192 | bytes 4958208 | tf_op jit(solution)/shard_map/while/body/eval_jaxpr/vmap(mks,msb->mkb)/dot_general | solution.py:64
  297.5 3.9 %gather_fusion = f32[24,12,128]{2,1,0:T(8,128)S(1)} fusion(f32[1024,12,128]{2,1,0:T(8,128)} %get-tuple-element.283, s32[1024]{0:T(1024)S(1)} %pad_clamp_fusion.2), kind=kCustom, calls=%fused_computation.clone.1 | custom fusion | bytes 295008 | tf_op jit(solution)/shard_map/while/body/eval_jaxpr/jit(_take)/gather | solution.py:84
  302.6 4.7 %multiply_reduce_fusion.2 = f32[2,3,1536,128]{3,2,1,0:T(8,128)S(1)} fusion(f32[2,3,3,1536]{3,2,1,0:T(4,128)S(1)} %copy.104, f32[2,3,3,128]{3,2,1,0:T(4,128)S(1)} %copy.105), kind=kLoop, calls=%fused_computation.1.clone.1 | loop fusion | flops 9437184 | bytes 4838400 | tf_op jit(solution)/shard_map/while/body/eval_jaxpr/vmap()/reduce_sum | solution.py:62
  307.4 4.2 %fusion.31 = f32[2,3,6,128]{3,2,1,0:T(8,128)S(1)} fusion(f32[2,3,1536,128]{3,2,1,0:T(8,128)S(1)} %multiply_reduce_fusion.2, f32[2,3,1,1536]{3,2,1,0:T(1,128)S(1)} %get-tuple-element.257, f32[2,3,1,1536]{3,2,1,0:T(1,128)S(1)} %get-tuple-element.258, f32[2,3,1,1536]{3,2,1,0:T(1,128)S(1)} %get-tuple-element.259, f32[2,3,3,1536]{3,2,1,0:T(4,128)S(1)} %broadcast_in_dim.68), kind=kOutput, calls=%fused_computation.2.clone.1 | convolution fusion | flops 86280192 | bytes 4958208 | tf_op jit(solution)/shard_map/while/body/eval_jaxpr/vmap(mks,msb->mkb)/dot_general | solution.py:64
  311.8 3.9 %gather_fusion = f32[24,12,128]{2,1,0:T(8,128)S(1)} fusion(f32[1024,12,128]{2,1,0:T(8,128)} %get-tuple-element.283, s32[1024]{0:T(1024)S(1)} %pad_clamp_fusion.2), kind=kCustom, calls=%fused_computation.clone.1 | custom fusion | bytes 295008 | tf_op jit(solution)/shard_map/while/body/eval_jaxpr/jit(_take)/gather | solution.py:84
  316.9 4.7 %multiply_reduce_fusion.2 = f32[2,3,1536,128]{3,2,1,0:T(8,128)S(1)} fusion(f32[2,3,3,1536]{3,2,1,0:T(4,128)S(1)} %copy.104, f32[2,3,3,128]{3,2,1,0:T(4,128)S(1)} %copy.105), kind=kLoop, calls=%fused_computation.1.clone.1 | loop fusion | flops 9437184 | bytes 4838400 | tf_op jit(solution)/shard_map/while/body/eval_jaxpr/vmap()/reduce_sum | solution.py:62
  321.7 4.2 %fusion.31 = f32[2,3,6,128]{3,2,1,0:T(8,128)S(1)} fusion(f32[2,3,1536,128]{3,2,1,0:T(8,128)S(1)} %multiply_reduce_fusion.2, f32[2,3,1,1536]{3,2,1,0:T(1,128)S(1)} %get-tuple-element.257, f32[2,3,1,1536]{3,2,1,0:T(1,128)S(1)} %get-tuple-element.258, f32[2,3,1,1536]{3,2,1,0:T(1,128)S(1)} %get-tuple-element.259, f32[2,3,3,1536]{3,2,1,0:T(4,128)S(1)} %broadcast_in_dim.68), kind=kOutput, calls=%fused_computation.2.clone.1 | convolution fusion | flops 86280192 | bytes 4958208 | tf_op jit(solution)/shard_map/while/body/eval_jaxpr/vmap(mks,msb->mkb)/dot_general | solution.py:64
  326.1 3.9 %gather_fusion = f32[24,12,128]{2,1,0:T(8,128)S(1)} fusion(f32[1024,12,128]{2,1,0:T(8,128)} %get-tuple-element.283, s32[1024]{0:T(1024)S(1)} %pad_clamp_fusion.2), kind=kCustom, calls=%fused_computation.clone.1 | custom fusion | bytes 295008 | tf_op jit(solution)/shard_map/while/body/eval_jaxpr/jit(_take)/gather | solution.py:84
  331.1 4.7 %multiply_reduce_fusion.2 = f32[2,3,1536,128]{3,2,1,0:T(8,128)S(1)} fusion(f32[2,3,3,1536]{3,2,1,0:T(4,128)S(1)} %copy.104, f32[2,3,3,128]{3,2,1,0:T(4,128)S(1)} %copy.105), kind=kLoop, calls=%fused_computation.1.clone.1 | loop fusion | flops 9437184 | bytes 4838400 | tf_op jit(solution)/shard_map/while/body/eval_jaxpr/vmap()/reduce_sum | solution.py:62
  335.9 4.2 %fusion.31 = f32[2,3,6,128]{3,2,1,0:T(8,128)S(1)} fusion(f32[2,3,1536,128]{3,2,1,0:T(8,128)S(1)} %multiply_reduce_fusion.2, f32[2,3,1,1536]{3,2,1,0:T(1,128)S(1)} %get-tuple-element.257, f32[2,3,1,1536]{3,2,1,0:T(1,128)S(1)} %get-tuple-element.258, f32[2,3,1,1536]{3,2,1,0:T(1,128)S(1)} %get-tuple-element.259, f32[2,3,3,1536]{3,2,1,0:T(4,128)S(1)} %broadcast_in_dim.68), kind=kOutput, calls=%fused_computation.2.clone.1 | convolution fusion | flops 86280192 | bytes 4958208 | tf_op jit(solution)/shard_map/while/body/eval_jaxpr/vmap(mks,msb->mkb)/dot_general | solution.py:64
  341.0 14.3 %all_gather.7 = f32[8,3,4096]{2,1,0:T(4,128)S(1)} all-gather(f32[1,3,4096]{2,1,0:T(4,128)S(1)} %copy.84), channel_id=1, replica_groups=mesh['tm'=8,'space'=32] {'tm'}, dimensions={0}, use_global_device_ids=true | all-gather | bytes 442368 | tf_op jit(solution)/shard_map/all_gather | solution.py:16
  356.1 0.9 reshape.103
  (325 shorter events, 17.8 us)
Async XLA Ops:
  6.5 2.5 copy-start
  6.5 95.5 %all-gather.2.cloned.1.call-start = ((), (), s32[]{:S(2)}) async-start(), calls=%async_computation | async-start | bytes 6488064 | tf_op jit(solution)/shard_map/all_gather | solution.py:78
  111.8 228.6 %copy-start.2 = (f32[3,3,1]{1,0,2:T(4,128)S(1)}, f32[3,3,1]{1,0,2:T(4,128)}, u32[]{:S(2)}) copy-start(f32[3,3,1]{1,0,2:T(4,128)} %constant.83) | copy-start | bytes 112
  111.8 244.1 %copy-start.1 = (f32[3,4096]{1,0:T(4,128)S(1)}, f32[3,4096]{1,0:T(4,128)}, u32[]{:S(2)}) copy-start(f32[3,4096]{1,0:T(4,128)} %param.12) | copy-start | bytes 147460
Sparse Core Ops, SparseCore 0:
  9.9 92.0 all-gather.1
where the time goes:
time: 365 us; the launch traced here: 364 us
  local copies, waits for them, and re-layouts  92.1 us (25%)
  waiting for transfers between devices  90.9 us (25%)
  other arithmetic  83 us (23%)
  matrix products  67.8 us (19%)
  blocking collectives  14.3 us (4%)
  between operations  13.5 us (4%)
    all_gather x1, waiting for transfers between devices, shards(): source_table = lax.all_gather(own_blocks, 'space', axis=0, tiled=True)  90.9 us
    reduce_sum x16, other arithmetic, block_velocity(): kernel = (jnp.sum(offset * offset, axis=1) + core_sq) ** (-1.5)  75.3 us
    dot_general x16, matrix products, block_velocity(): jnp.einsum('mks,msb->mkb', weights, kernel, precision=lax.Precision.HIGHEST)  67.3 us
    gather x16, local copies, waits for them, and re-layouts, one_group(): group_sources = jnp.take(source_table, group_slots.reshape(-1), axis=0)  63.1 us
    all_gather x1, blocking collectives, entering(): pieces = lax.all_gather(value, axis)  14.3 us
    dynamic_slice x16, local copies, waits for them, and re-layouts, shards(): lax.map(one_group, (my_lists.reshape(steps_count, group_size, list_len),...  11.3 us
    while x1, local copies, waits for them, and re-layouts, shards(): lax.map(one_group, (my_lists.reshape(steps_count, group_size, list_len),...  9.79 us
  transfers between devices with their start and end apart: 1, of which 1 were waited for; matrix products, arithmetic and copies ran while one was open for 1% of the time, Pallas kernels for 0%

commit v1 on v0

v1 whole, which is shorter than its diff:
```python
import math

import jax
import jax.numpy as jnp
import numpy as np
from jax import lax
from jax.experimental import pallas as pl
from jax.experimental.pallas import tpu as pltpu
from jax.sharding import PartitionSpec as P

core_sq = 0.25
step_size = 1.0
LANES = 128
ROWS = 16
bf16 = jnp.bfloat16
f32 = jnp.float32


def radau_matrix():
    sqrt_six = math.sqrt(6.0)
    return np.array(
        [
            [
                (88.0 - 7.0 * sqrt_six) / 360.0,
                (296.0 - 169.0 * sqrt_six) / 1800.0,
                (-2.0 + 3.0 * sqrt_six) / 225.0,
            ],
            [
                (296.0 + 169.0 * sqrt_six) / 1800.0,
                (88.0 + 7.0 * sqrt_six) / 360.0,
                (-2.0 - 3.0 * sqrt_six) / 225.0,
            ],
            [(16.0 - sqrt_six) / 36.0, (16.0 + sqrt_six) / 36.0, 1.0 / 9.0],
        ]
    )


def pieces(value):
    first = value.astype(bf16)
    rest = value - first.astype(f32)
    second = rest.astype(bf16)
    third = (rest - second.astype(f32)).astype(bf16)
    return first, second, third


def norm_rows(rows, extra):
    square = rows * rows
    norm = square + pltpu.roll(square, ROWS - 1, 0) + pltpu.roll(square, ROWS - 2, 0) + extra
    first, second, third = [piece.astype(f32) for piece in pieces(norm)]
    place = lax.broadcasted_iota(jnp.int32, (ROWS, LANES), 0) % 3
    return jnp.where(
        place == 0,
        first,
        jnp.where(place == 1, pltpu.roll(second, 1, 0), pltpu.roll(third, 2, 0)),
    )


def cross(former, latter):
    return [
        former[1] * latter[2] - former[2] * latter[1],
        former[2] * latter[0] - former[0] * latter[2],
        former[0] * latter[1] - former[1] * latter[0],
    ]


def source_features(rows, feature_ref, weight_ref, slot):
    first, second, third = [(-2.0 * piece.astype(f32)).astype(bf16) for piece in pieces(rows)]
    norms = norm_rows(rows, core_sq).astype(bf16)
    ones = jnp.ones((ROWS, LANES), bf16)
    stacked = jnp.concatenate([first, second, first, second, third, first, norms, ones], 0)
    feature_ref[slot] = stacked.T
    strength = [rows[9 + c : 10 + c] for c in range(3)]
    blank = jnp.zeros((2, LANES), f32)
    for m in range(3):
        place = [rows[3 * m + c : 3 * m + c + 1] for c in range(3)]
        weights = jnp.concatenate(strength + cross(place, strength) + [blank], 0)
        parts = [piece.astype(f32) for piece in pieces(weights)]
        weight_ref[slot, m] = jnp.concatenate(parts + [jnp.zeros((8, LANES), f32)], 0).astype(bf16)


def target_features(rows):
    first, second, third = [piece.astype(f32) for piece in pieces(rows)]
    norms = norm_rows(rows, 0.0)
    place = lax.broadcasted_iota(jnp.int32, (ROWS, LANES), 0)
    ones = jnp.ones((ROWS, LANES), f32)
    groups = (first, first, second, second, first, third, ones, norms)
    made = []
    for m in range(3):
        node = (place >= 3 * m) & (place < 3 * m + 3)
        made.append(jnp.concatenate([jnp.where(node, g, 0.0).astype(bf16) for g in groups], 0))
    return made


def gather_kernel(pick_ref, own_ref, send_ref):
    def one(d, _):
        send_ref[d, 0:12] = own_ref[pick_ref[0, d], 0:12]
        send_ref[d, 12:24] = own_ref[pick_ref[1, d], 0:12]
        return 0

    lax.fori_loop(0, send_ref.shape[0], one, 0)


def rates_kernel(
    table_ref, live_ref, own_ref, far_ref, start_ref, base_ref, step_ref, feature_ref, weight_ref
):
    blocks = own_ref.shape[0]
    shards_count = far_ref.shape[0]
    list_len = table_ref.shape[0] // blocks
    radau = radau_matrix() * step_size

    def own_source(i, _):
        source_features(own_ref[i], feature_ref, weight_ref, i)
        return 0

    def far_source(i, _):
        blank = jnp.zeros((4, LANES), f32)
        for k in range(2):
            rows = jnp.concatenate([far_ref[i, 12 * k : 12 * k + 12], blank], 0)
            source_features(rows, feature_ref, weight_ref, blocks + 2 * i + k)
        return 0

    lax.fori_loop(0, blocks, own_source, 0)
    lax.fori_loop(0, shards_count, far_source, 0)
    live = live_ref[0]

    def pair(i, _):
        ids = (2 * i, 2 * i + 1)
        rows = [own_ref[t] for t in ids]
        targets = [target_features(r) for r in rows]
        slots = [[table_ref[t * list_len + j] for j in range(list_len)] for t in ids]
        zero = jnp.zeros((LANES, LANES), bf16)
        velocity = ([], [])
        for m in range(3):
            both = jnp.concatenate(
                [
                    jnp.concatenate([targets[0][m], zero], 1),
                    jnp.concatenate([zero, targets[1][m]], 1),
                ],
                0,
            )
            total = jnp.zeros((64, 2 * LANES), f32)
            for j in range(0, list_len, 2):
                features = jnp.concatenate(
                    [
                        jnp.concatenate([feature_ref[slots[0][q]], feature_ref[slots[1][q]]], 1)
                        for q in (j, j + 1)
                    ],
                    0,
                )
                weights = jnp.concatenate(
                    [
                        jnp.concatenate([weight_ref[s[j], m], weight_ref[s[j + 1], m]], 1)
                        for s in slots
                    ],
                    0,
                )
                squares = jnp.dot(features, both, preferred_element_type=f32)
                inverse = lax.rsqrt(squares)
                kernel = inverse * inverse * inverse
                high = kernel.astype(bf16)
                low = (kernel - high.astype(f32)).astype(bf16)
                total = total + jnp.dot(weights, high, preferred_element_type=f32)
                total = total + jnp.dot(weights, low, preferred_element_type=f32)
            for q in range(2):
                mine = total[32 * q : 32 * q + 32, LANES * q : LANES * q + LANES]
                sums = mine[0:8] + mine[8:16] + mine[16:24]
                place = [rows[q][3 * m + c : 3 * m + c + 1] for c in range(3)]
                spread = cross(place, [sums[c : c + 1] for c in range(3)])
                velocity[q].append(
                    [(spread[c] - sums[3 + c : 4 + c]) * (-0.25 / math.pi) for c in range(3)]
                )
        for q in range(2):
            t = ids[q]
            on = jnp.where(t < live, 1.0, 0.0).astype(f32)
            lanes = pl.ds(pl.multiple_of(t * LANES, LANES), LANES)
            start = start_ref[:, lanes]
            for k in range(3):
                step = [
                    sum(float(radau[k, n]) * velocity[q][n][c] for n in range(3)) * on
                    for c in range(3)
                ]
                step = jnp.concatenate(step, 0)
                base_ref[3 * k : 3 * k + 3, lanes] = start + step
                if k == 2:
                    step_ref[:, lanes] = step
        return 0

    lax.fori_loop(0, blocks // 2, pair, 0)


def vmem():
    return pl.BlockSpec(memory_space=pltpu.VMEM)


def smem():
    return pl.BlockSpec(memory_space=pltpu.SMEM)


def shards(node_states, strengths, start_state, lists, counts):
    groups = lax.axis_size("space")
    slices = lax.axis_size("tm")
    rank = lax.axis_index("space")
    blocks = lists.shape[0] // groups
    list_len = lists.shape[1]
    particles = node_states.shape[2]
    own = jnp.concatenate([node_states[0], strengths, jnp.zeros((4, particles), f32)], axis=0)
    own = own.reshape(ROWS, blocks, LANES).transpose(1, 0, 2)

    owner, block = lists // blocks, lists % blocks
    mine = owner == rank
    lowest = jnp.min(jnp.where(mine, block, blocks - 1).reshape(groups, -1), axis=1)
    highest = jnp.max(jnp.where(mine, block, 0).reshape(groups, -1), axis=1)
    send = pl.pallas_call(
        gather_kernel,
        out_shape=jax.ShapeDtypeStruct((groups, 24, LANES), f32),
        in_specs=[smem(), vmem()],
        out_specs=vmem(),
        name="gather_blocks",
    )(jnp.stack([lowest, highest]), own)
    far = lax.all_to_all(send, "space", 0, 0, tiled=True)

    my_lists = lax.dynamic_slice_in_dim(lists, rank * blocks, blocks, 0)
    owner, block = my_lists.reshape(-1) // blocks, my_lists.reshape(-1) % blocks
    from_shard = owner[None, :] == jnp.arange(groups, dtype=jnp.int32)[:, None]
    first = jnp.min(jnp.where(from_shard, block[None, :], blocks - 1), axis=1)
    first = jnp.sum(jnp.where(from_shard, first[:, None], 0), axis=0)
    table = jnp.where(
        owner == rank, block, blocks + 2 * owner + (block != first).astype(jnp.int32)
    )
    live = lax.dynamic_slice_in_dim(counts, rank, 1, 0)

    base, step = pl.pallas_call(
        rates_kernel,
        out_shape=(
            jax.ShapeDtypeStruct((9, particles), f32),
            jax.ShapeDtypeStruct((3, particles), f32),
        ),
        in_specs=[smem(), smem(), vmem(), vmem(), vmem()],
        out_specs=(vmem(), vmem()),
        scratch_shapes=[
            pltpu.VMEM((blocks + 2 * groups, LANES, LANES), bf16),
            pltpu.VMEM((blocks + 2 * groups, 3, 32, LANES), bf16),
        ],
        compiler_params=pltpu.CompilerParams(vmem_limit_bytes=56 << 20),
        name="rates",
    )(table, live, own, far, start_state)

    def earlier(value, shift):
        return lax.ppermute(value, "tm", [(i, i + shift) for i in range(slices - shift)])

    carried = earlier(step, 1)
    span, shift = step + carried, 2
    while shift < slices:
        got = earlier(span, shift)
        carried, span, shift = carried + got, span + got, 2 * shift
    new = base.reshape(3, 3, particles) + carried[None]
    return new.reshape(1, 9, particles)


def solution(mesh):
    return jax.shard_map(
        shards,
        mesh=mesh,
        in_specs=(P("tm", None, "space"), P(None, "space"), P(None, "space"), P(), P()),
        out_specs=P("tm", None, "space"),
        check_vma=False,
    )
```

time: 365 us -> 92.8 us (0.25)
  the two profiles are of different devices: /device:TPU:1 before, /device:TPU:16 now
where the time goes in v1:
time: 92.8 us; the launch traced here: 92.3 us
  Pallas kernels  38.7 us (42%)
  waiting for transfers between devices  25.4 us (27%)
  starting transfers between devices  17.7 us (19%)
  local copies, waits for them, and re-layouts  6.04 us (7%)
  other arithmetic  4.28 us (5%)
    pallas_call x1, Pallas kernels, shards(): pl.pallas_call(rates_kernel, out_shape=(jax.ShapeDtypeStruct((9, particle...  36.8 us
    ppermute x3, waiting for transfers between devices, earlier(): lax.ppermute(value, 'tm', [(i, i + shift) for i in range(slices - shift)])  13.2 us
    all_to_all x1, waiting for transfers between devices, shards(): far = lax.all_to_all(send, 'space', 0, 0, tiled=True)  12.2 us
    all_to_all x1, starting transfers between devices, shards(): far = lax.all_to_all(send, 'space', 0, 0, tiled=True)  11.3 us
    ppermute x3, starting transfers between devices, earlier(): lax.ppermute(value, 'tm', [(i, i + shift) for i in range(slices - shift)])  6.39 us
    unnamed x8, local copies, waits for them, and re-layouts  2.25 us
    pallas_call x1, Pallas kernels, shards(): pl.pallas_call(gather_kernel, out_shape=jax.ShapeDtypeStruct((groups, 24,...  1.96 us
  transfers between devices with their start and end apart: 4, of which 4 were waited for; matrix products, arithmetic and copies ran while one was open for 3% of the time, Pallas kernels for 0%

profile of v1, /device:TPU:16, one launch (start us, length us, event | category | flops | bytes accessed | tf_op | source)
XLA Modules:
  0.0 92.3 jit_solution(9361994779000183663)
XLA Ops:
  0.0 0.9 %select_reduce_fusion.1 = (s32[1024]{0:T(1024)S(1)}, s32[1024]{0:T(1024)S(1)}) fusion(s32[1024,12]{0,1:T(8,128)} %param.8, s32[]{:T(128)S(6)} %axis_index.12), kind=kLoop, calls=%fused_computation.10 | loop fusion | flops 292864 | bytes 57348 | tf_op jit(solution)/shard_map/reduce_min | solution.py:211
  0.9 0.1 reduce_min.27
  1.0 0.1 reduce_max.14
  1.1 0.0 copy-start.2
  1.1 1.0 %copy.11 = f32[9,32,128]{2,0,1:T(8,128)S(1)} copy(f32[9,32,128]{2,1,0:T(8,128)} %bitcast.8) | data formatting | bytes 294912 | tf_op jit(solution)/shard_map/concatenate | solution.py:206
  2.1 0.1 pad.4.clone
  2.2 0.1 reduce_min.28
  2.3 0.1 reduce_max.18
  2.4 0.6 pad_add_fusion.pick_ref
  3.0 0.0 copy-done.2
  3.0 0.8 maximum_bitcast_fusion.own_ref
  3.8 2.0 %gather_blocks.1 = f32[32,24,128]{2,1,0:T(8,128)} custom-call(s32[2,32]{1,0:T(2,128)} %pad_add_fusion.pick_ref, f32[32,16,128]{2,1,0:T(8,128)} %maximum_bitcast_fusion.own_ref), custom_call_target="tpu_custom_call" | custom-call | tf_op jit(solution)/shard_map/gather_blocks/pallas_call | solution.py:213
  5.8 11.3 %all-to-all-start = ((f32[32,24,128]{2,1,0:T(8,128)}), f32[32,24,128]{2,1,0:T(8,128)S(1)}, u32[]{:S(2)}, u32[]{:S(2)}) async-start(f32[32,24,128]{2,1,0:T(8,128)} %gather_blocks.1), calls=%async_computation | async-start | bytes 786432 | tf_op jit(solution)/shard_map/all_to_all | solution.py:220
  17.1 0.8 constant_dynamic-slice_fusion
  17.9 0.1 copy.10
  18.0 0.1 reshape.72
  18.1 0.0 copy-start.3
  18.1 0.6 copy-done.3
  18.7 0.6 dynamic_slice.7.live_ref
  19.4 0.1 select_reduce_fusion.3
  19.5 0.1 select_reduce_fusion.2
  19.6 0.6 add_select_fusion.4.table_ref
  20.2 12.2 %all-to-all-done.far_ref = f32[32,24,128]{2,1,0:T(8,128)S(1)} async-done(((f32[32,24,128]{2,1,0:T(8,128)}), f32[32,24,128]{2,1,0:T(8,128)S(1)}, u32[]{:S(2)}, u32[]{:S(2)}) %all-to-all-start) | async-done | bytes 393248 | tf_op jit(solution)/shard_map/all_to_all | solution.py:220
  32.4 0.0 copy-start
  32.4 0.7 copy-done
  33.2 36.8 %rates.1 = (f32[9,4096]{1,0:T(8,128)}, f32[3,4096]{1,0:T(4,128)}) custom-call(s32[384]{0:T(512)} %add_select_fusion.4.table_ref, s32[1]{0:T(128)} %dynamic_slice.7.live_ref, f32[32,16,128]{2,1,0:T(8,128)} %maximum_bitcast_fusion.own_ref, f32[32,24,128]{2,1,0:T(8,128)} %copy-done, f32[3,4096]{1,0:T(4,128)} %start_ref.1), custom_call_target="tpu_custom_call" | custom-call | tf_op jit(solution)/shard_map/rates/pallas_call | solution.py:232
  69.9 1.9 %collective-permute-start = (f32[3,4096]{1,0:T(4,128)}, f32[3,4096]{1,0:T(4,128)S(1)}, u32[]{:S(2)}, u32[]{:S(2)}) collective-permute-start(f32[3,4096]{1,0:T(4,128)} %get-tuple-element.8), channel_id=1, source_target_pairs={{0,32},{32,64},{64,96},{96,128},{128,160},{160,192},{192,224},{1,3... | collective-permute-start | bytes 147464 | tf_op jit(solution)/shard_map/ppermute | solution.py:249
  71.9 3.9 %collective-permute-done = f32[3,4096]{1,0:T(4,128)S(1)} collective-permute-done((f32[3,4096]{1,0:T(4,128)}, f32[3,4096]{1,0:T(4,128)S(1)}, u32[]{:S(2)}, u32[]{:S(2)}) %collective-permute-start) | collective-permute-done | bytes 49184 | tf_op jit(solution)/shard_map/ppermute | solution.py:249
  75.7 0.9 add.67
  76.6 3.2 %collective-permute-start.1 = (f32[3,4096]{1,0:T(4,128)S(1)}, f32[3,4096]{1,0:T(4,128)S(1)}, u32[]{:S(2)}, u32[]{:S(2)}) collective-permute-start(f32[3,4096]{1,0:T(4,128)S(1)} %add.67), channel_id=1, source_target_pairs={{0,64},{32,96},{64,128},{96,160},{128,192},{160,224},{1,65},{33,97... | collective-permute-start | bytes 147464 | tf_op jit(solution)/shard_map/ppermute | solution.py:249
  79.8 3.0 %collective-permute-done.1 = f32[3,4096]{1,0:T(4,128)S(1)} collective-permute-done((f32[3,4096]{1,0:T(4,128)S(1)}, f32[3,4096]{1,0:T(4,128)S(1)}, u32[]{:S(2)}, u32[]{:S(2)}) %collective-permute-start.1) | collective-permute-done | bytes 49184 | tf_op jit(solution)/shard_map/ppermute | solution.py:249
  82.8 1.3 %collective-permute-start.2 = (f32[3,4096]{1,0:T(4,128)S(1)}, f32[3,4096]{1,0:T(4,128)S(1)}, u32[]{:S(2)}, u32[]{:S(2)}) collective-permute-start(f32[3,4096]{1,0:T(4,128)S(1)} %add.69), channel_id=1, source_target_pairs={{0,128},{32,160},{64,192},{96,224},{1,129},{33,161},{65,193},{97,2... | collective-permute-start | bytes 147464 | tf_op jit(solution)/shard_map/ppermute | solution.py:249
  84.1 6.4 %collective-permute-done.2 = f32[3,4096]{1,0:T(4,128)S(1)} collective-permute-done((f32[3,4096]{1,0:T(4,128)S(1)}, f32[3,4096]{1,0:T(4,128)S(1)}, u32[]{:S(2)}, u32[]{:S(2)}) %collective-permute-start.2) | collective-permute-done | bytes 49184 | tf_op jit(solution)/shard_map/ppermute | solution.py:249
  90.5 0.0 copy-start.1
  90.5 0.1 add.72
  90.6 0.9 copy-done.1
  91.5 0.8 copy.12
  (6 shorter events, 0.1 us)
Async XLA Ops:
  1.1 1.9 %copy-start.2 = (f32[3,4096]{1,0:T(4,128)S(1)}, f32[3,4096]{1,0:T(4,128)}, u32[]{:S(2)}) copy-start(f32[3,4096]{1,0:T(4,128)} %param.6) | copy-start | bytes 147460
  5.8 26.7 %all-to-all-start = ((f32[32,24,128]{2,1,0:T(8,128)}), f32[32,24,128]{2,1,0:T(8,128)S(1)}, u32[]{:S(2)}, u32[]{:S(2)}) async-start(f32[32,24,128]{2,1,0:T(8,128)} %gather_blocks.1), calls=%async_computation | async-start | bytes 786432 | tf_op jit(solution)/shard_map/all_to_all | solution.py:220
  18.1 0.7 copy-start.3
  32.4 0.7 copy-start
  69.9 5.8 %collective-permute-start = (f32[3,4096]{1,0:T(4,128)}, f32[3,4096]{1,0:T(4,128)S(1)}, u32[]{:S(2)}, u32[]{:S(2)}) collective-permute-start(f32[3,4096]{1,0:T(4,128)} %get-tuple-element.8), channel_id=1, source_target_pairs={{0,32},{32,64},{64,96},{96,128},{128,160},{160,192},{192,224},{1,3... | collective-permute-start | bytes 147464 | tf_op jit(solution)/shard_map/ppermute | solution.py:249
  76.6 6.2 %collective-permute-start.1 = (f32[3,4096]{1,0:T(4,128)S(1)}, f32[3,4096]{1,0:T(4,128)S(1)}, u32[]{:S(2)}, u32[]{:S(2)}) collective-permute-start(f32[3,4096]{1,0:T(4,128)S(1)} %add.67), channel_id=1, source_target_pairs={{0,64},{32,96},{64,128},{96,160},{128,192},{160,224},{1,65},{33,97... | collective-permute-start | bytes 147464 | tf_op jit(solution)/shard_map/ppermute | solution.py:249
  82.8 7.7 %collective-permute-start.2 = (f32[3,4096]{1,0:T(4,128)S(1)}, f32[3,4096]{1,0:T(4,128)S(1)}, u32[]{:S(2)}, u32[]{:S(2)}) collective-permute-start(f32[3,4096]{1,0:T(4,128)S(1)} %add.69), channel_id=1, source_target_pairs={{0,128},{32,160},{64,192},{96,224},{1,129},{33,161},{65,193},{97,2... | collective-permute-start | bytes 147464 | tf_op jit(solution)/shard_map/ppermute | solution.py:249
  90.5 1.0 %copy-start.1 = (f32[9,4096]{1,0:T(8,128)S(1)}, f32[9,4096]{1,0:T(8,128)}, u32[]{:S(2)}) copy-start(f32[9,4096]{1,0:T(8,128)} %get-tuple-element.7) | copy-start | bytes 442372

commit v2 on v1

v2 whole, which is shorter than its diff:
```python
import functools
import math

import jax
import jax.numpy as jnp
import numpy as np
from jax import lax
from jax.experimental import pallas as pl
from jax.experimental.pallas import tpu as pltpu
from jax.sharding import PartitionSpec as P

core_sq = 0.25
step_size = 1.0
LANES = 128
ROWS = 16
MOST_EARLY = 3
bf16 = jnp.bfloat16
f32 = jnp.float32


def radau_matrix():
    sqrt_six = math.sqrt(6.0)
    return np.array(
        [
            [
                (88.0 - 7.0 * sqrt_six) / 360.0,
                (296.0 - 169.0 * sqrt_six) / 1800.0,
                (-2.0 + 3.0 * sqrt_six) / 225.0,
            ],
            [
                (296.0 + 169.0 * sqrt_six) / 1800.0,
                (88.0 + 7.0 * sqrt_six) / 360.0,
                (-2.0 - 3.0 * sqrt_six) / 225.0,
            ],
            [(16.0 - sqrt_six) / 36.0, (16.0 + sqrt_six) / 36.0, 1.0 / 9.0],
        ]
    )


def pieces(value):
    first = value.astype(bf16)
    rest = value - first.astype(f32)
    second = rest.astype(bf16)
    third = (rest - second.astype(f32)).astype(bf16)
    return first, second, third


def norm_rows(rows, extra):
    square = rows * rows
    norm = square + pltpu.roll(square, ROWS - 1, 0) + pltpu.roll(square, ROWS - 2, 0) + extra
    first, second, third = [piece.astype(f32) for piece in pieces(norm)]
    place = lax.broadcasted_iota(jnp.int32, (ROWS, LANES), 0) % 3
    return jnp.where(
        place == 0,
        first,
        jnp.where(place == 1, pltpu.roll(second, 1, 0), pltpu.roll(third, 2, 0)),
    )


def cross(former, latter):
    return [
        former[1] * latter[2] - former[2] * latter[1],
        former[2] * latter[0] - former[0] * latter[2],
        former[0] * latter[1] - former[1] * latter[0],
    ]


def source_features(rows, feature_ref, weight_ref, slot):
    first, second, third = [(-2.0 * piece.astype(f32)).astype(bf16) for piece in pieces(rows)]
    norms = norm_rows(rows, core_sq).astype(bf16)
    ones = jnp.ones((ROWS, LANES), bf16)
    stacked = jnp.concatenate([first, second, first, second, third, first, norms, ones], 0)
    feature_ref[slot] = stacked.T
    strength = [rows[9 + c : 10 + c] for c in range(3)]
    blank = jnp.zeros((2, LANES), f32)
    for m in range(3):
        place = [rows[3 * m + c : 3 * m + c + 1] for c in range(3)]
        weights = jnp.concatenate(strength + cross(place, strength) + [blank], 0)
        parts = [piece.astype(f32) for piece in pieces(weights)]
        weight_ref[slot, m] = jnp.concatenate(parts + [jnp.zeros((8, LANES), f32)], 0).astype(bf16)


def target_features(rows, target_ref, t):
    first, second, third = [piece.astype(f32) for piece in pieces(rows)]
    norms = norm_rows(rows, 0.0)
    place = lax.broadcasted_iota(jnp.int32, (ROWS, LANES), 0)
    ones = jnp.ones((ROWS, LANES), f32)
    groups = (first, first, second, second, first, third, ones, norms)
    for m in range(3):
        node = (place >= 3 * m) & (place < 3 * m + 3)
        target_ref[t, m] = jnp.concatenate(
            [jnp.where(node, g, 0.0).astype(bf16) for g in groups], 0
        )


def lanes_of(t):
    return pl.ds(pl.multiple_of(t * LANES, LANES), LANES)


def pair_sums(table_ref, target_ref, feature_ref, weight_ref, i, m, begin, end):
    list_len = table_ref.shape[0] // target_ref.shape[0]
    ids = (2 * i, 2 * i + 1)
    zero = jnp.zeros((LANES, LANES), bf16)
    both = jnp.concatenate(
        [
            jnp.concatenate([target_ref[ids[0], m], zero], 1),
            jnp.concatenate([zero, target_ref[ids[1], m]], 1),
        ],
        0,
    )
    total = jnp.zeros((64, 2 * LANES), f32)
    for j in range(begin, end, 2):
        slots = [[table_ref[t * list_len + q] for q in (j, j + 1)] for t in ids]
        features = jnp.concatenate(
            [
                jnp.concatenate([feature_ref[slots[0][q]], feature_ref[slots[1][q]]], 1)
                for q in range(2)
            ],
            0,
        )
        weights = jnp.concatenate(
            [jnp.concatenate([weight_ref[s[0], m], weight_ref[s[1], m]], 1) for s in slots], 0
        )
        squares = jnp.dot(features, both, preferred_element_type=f32)
        inverse = lax.rsqrt(squares)
        kernel = inverse * inverse * inverse
        high = kernel.astype(bf16)
        low = (kernel - high.astype(f32)).astype(bf16)
        total = total + jnp.dot(weights, high, preferred_element_type=f32)
        total = total + jnp.dot(weights, low, preferred_element_type=f32)
    sums = []
    for q in range(2):
        mine = total[32 * q : 32 * q + 32, LANES * q : LANES * q + LANES]
        sums.append(mine[0:8] + mine[8:16] + mine[16:24])
    return sums


def fetch(pairs, sems):
    copies = [pltpu.make_async_copy(a, b, sems.at[k]) for k, (a, b) in enumerate(pairs)]
    for copy in copies:
        copy.start()
    return copies


def gather_kernel(pick_ref, node_in, strength_in, send_ref, node_ref, strength_ref, sems):
    for copy in fetch(((node_in, node_ref), (strength_in, strength_ref)), sems):
        copy.wait()

    def one(d, _):
        for k in range(2):
            lanes = lanes_of(pick_ref[k, d])
            send_ref[d, 12 * k : 12 * k + 9] = node_ref[:, pick_ref[k, d], :]
            send_ref[d, 12 * k + 9 : 12 * k + 12] = strength_ref[:, lanes]
        return 0

    lax.fori_loop(0, send_ref.shape[0], one, 0, unroll=4)


def near_kernel(
    table_ref,
    early_ref,
    node_in,
    strength_in,
    feature_out,
    weight_out,
    target_out,
    part_out,
    feature_ref,
    weight_ref,
    target_ref,
    part_ref,
    node_ref,
    strength_ref,
    sems,
):
    blocks = part_ref.shape[0]
    for copy in fetch(((node_in, node_ref), (strength_in, strength_ref)), sems):
        copy.wait()

    def prepare(t, _):
        lanes = lanes_of(t)
        rows = jnp.concatenate(
            [node_ref[:, t, :], strength_ref[:, lanes], jnp.zeros((4, LANES), f32)], 0
        )
        source_features(rows, feature_ref, weight_ref, t)
        target_features(rows, target_ref, t)
        return 0

    lax.fori_loop(0, blocks, prepare, 0, unroll=4)
    kept = ((feature_ref, feature_out), (weight_ref, weight_out), (target_ref, target_out))
    copies = fetch(kept, sems)

    def pair(i, _):
        for steps in range(MOST_EARLY + 1):

            @pl.when(early_ref[i] == steps)
            def _():
                for m in range(3):
                    sums = pair_sums(
                        table_ref, target_ref, feature_ref, weight_ref, i, m, 0, 2 * steps
                    )
                    for q in range(2):
                        part_ref[2 * i + q, m] = sums[q]

        return 0

    lax.fori_loop(0, blocks // 2, pair, 0)
    copies.append(pltpu.make_async_copy(part_ref, part_out, sems.at[3]))
    copies[3].start()
    for copy in copies:
        copy.wait()


def rest_kernel(
    table_ref,
    early_ref,
    live_ref,
    far_ref,
    near_feature,
    near_weight,
    near_target,
    near_part,
    node_in,
    start_in,
    base_out,
    step_ref,
    feature_ref,
    weight_ref,
    target_ref,
    part_ref,
    node_ref,
    start_ref,
    base_ref,
    sems,
):
    blocks = part_ref.shape[0]
    list_len = table_ref.shape[0] // blocks
    radau = radau_matrix() * step_size

    def far_source(i, _):
        blank = jnp.zeros((4, LANES), f32)
        for k in range(2):
            rows = jnp.concatenate([far_ref[i, 12 * k : 12 * k + 12], blank], 0)
            source_features(rows, feature_ref, weight_ref, blocks + 2 * i + k)
        return 0

    kept = (
        (near_feature, feature_ref.at[0:blocks]),
        (near_weight, weight_ref.at[0:blocks]),
        (near_target, target_ref),
        (near_part, part_ref),
        (node_in, node_ref),
        (start_in, start_ref),
    )
    copies = fetch(kept, sems)
    lax.fori_loop(0, far_ref.shape[0], far_source, 0, unroll=2)
    for copy in copies:
        copy.wait()
    live = live_ref[0]

    def pair(i, _):
        for steps in range(MOST_EARLY + 1):

            @pl.when(early_ref[i] == steps)
            def _():
                finish(i, 2 * steps)

        return 0

    def finish(i, begin):
        lanes = [lanes_of(2 * i + q) for q in range(2)]
        rows = [node_ref[:, 2 * i + q, :] for q in range(2)]
        velocity = ([], [])
        for m in range(3):
            both = pair_sums(
                table_ref, target_ref, feature_ref, weight_ref, i, m, begin, list_len
            )
            for q in range(2):
                sums = both[q] + part_ref[2 * i + q, m]
                place = [rows[q][3 * m + c : 3 * m + c + 1] for c in range(3)]
                spread = cross(place, [sums[c : c + 1] for c in range(3)])
                velocity[q].append(
                    [(spread[c] - sums[3 + c : 4 + c]) * (-0.25 / math.pi) for c in range(3)]
                )
        for q in range(2):
            on = jnp.where(2 * i + q < live, 1.0, 0.0).astype(f32)
            start = start_ref[:, lanes[q]]
            for k in range(3):
                step = [
                    sum(float(radau[k, n]) * velocity[q][n][c] for n in range(3)) * on
                    for c in range(3)
                ]
                for c in range(3):
                    base_ref[3 * k + c, pl.ds(2 * i + q, 1), :] = start[c : c + 1] + step[c]
                    if k == 2:
                        step_ref[c, pl.ds(2 * i + q, 1), :] = step[c]

    half = blocks // 2
    copies = []
    for k in range(2):
        lax.fori_loop(k * half // 2, (k + 1) * half // 2, pair, 0)
        rows = pl.ds(k * half, half)
        copy = pltpu.make_async_copy(base_ref.at[:, rows], base_out.at[:, rows], sems.at[k])
        copy.start()
        copies.append(copy)
    for copy in copies:
        copy.wait()


def hbm():
    return pl.BlockSpec(memory_space=pltpu.HBM)


def in_hbm(value):
    return pltpu.with_memory_space_constraint(value, pltpu.HBM)


def vmem():
    return pl.BlockSpec(memory_space=pltpu.VMEM)


def smem():
    return pl.BlockSpec(memory_space=pltpu.SMEM)


def sum_kernel(shifts, base_in, other_ref, *refs):
    got_refs, (out_ref, base_ref, sems) = refs[:-3], refs[-3:]
    (copy,) = fetch(((base_in, base_ref),), sems)
    rank = lax.axis_index("tm")

    def keep(value, k):
        return jnp.where((rank ^ k) < rank, 1.0, 0.0).astype(f32) * value

    carried = keep(other_ref[...], 1)
    for k, ref in zip(shifts, got_refs):
        carried = carried + keep(ref[...], k)
    copy.wait()
    for m in range(3):
        out_ref[3 * m : 3 * m + 3] = base_ref[3 * m : 3 * m + 3] + carried


def add_earlier(base, step, slices):
    def swap(value, k):
        return lax.ppermute(value, "tm", [(i, i ^ k) for i in range(slices)])

    other = swap(step, 1)
    chip = step + other
    shifts = tuple(range(2, slices, 2))
    got = [swap(chip, k) for k in shifts]
    return pl.pallas_call(
        functools.partial(sum_kernel, shifts),
        out_shape=jax.ShapeDtypeStruct(base.shape, f32),
        in_specs=[hbm()] + [vmem()] * (1 + len(got)),
        out_specs=vmem(),
        scratch_shapes=[pltpu.VMEM(base.shape, f32), pltpu.SemaphoreType.DMA((1,))],
        compiler_params=pltpu.CompilerParams(vmem_limit_bytes=8 << 20),
        name="add_earlier",
    )(in_hbm(base), other, *got)


def shards(node_states, strengths, start_state, lists, counts):
    groups = lax.axis_size("space")
    slices = lax.axis_size("tm")
    rank = lax.axis_index("space")
    blocks = lists.shape[0] // groups
    list_len = lists.shape[1]
    nodes = in_hbm(node_states.reshape(9, blocks, LANES))
    strengths, start_state = in_hbm(strengths), in_hbm(start_state)

    owner, block = lists // blocks, lists % blocks
    mine = owner == rank
    lowest = jnp.min(jnp.where(mine, block, blocks - 1).reshape(groups, -1), axis=1)
    highest = jnp.max(jnp.where(mine, block, 0).reshape(groups, -1), axis=1)
    send = pl.pallas_call(
        gather_kernel,
        out_shape=jax.ShapeDtypeStruct((groups, 24, LANES), f32),
        in_specs=[smem(), hbm(), hbm()],
        out_specs=vmem(),
        scratch_shapes=[
            pltpu.VMEM((9, blocks, LANES), f32),
            pltpu.VMEM((3, blocks * LANES), f32),
            pltpu.SemaphoreType.DMA((2,)),
        ],
        compiler_params=pltpu.CompilerParams(vmem_limit_bytes=8 << 20),
        name="gather_blocks",
    )(jnp.stack([lowest, highest]), nodes, strengths)
    far = lax.all_to_all(send, "space", 0, 0, tiled=True)

    my_lists = lax.dynamic_slice_in_dim(lists, rank * blocks, blocks, 0)
    owner, block = my_lists.reshape(-1) // blocks, my_lists.reshape(-1) % blocks
    from_shard = owner[None, :] == jnp.arange(groups, dtype=jnp.int32)[:, None]
    first = jnp.min(jnp.where(from_shard, block[None, :], blocks - 1), axis=1)
    first = jnp.sum(jnp.where(from_shard, first[:, None], 0), axis=0)
    slot = jnp.where(
        owner == rank, block, blocks + 2 * owner + (block != first).astype(jnp.int32)
    ).reshape(blocks, list_len)
    near = (slot < blocks).astype(jnp.int32)
    order = jnp.arange(list_len, dtype=jnp.int32)
    ahead = order[None, :] < order[:, None]
    near_ahead = jnp.sum(jnp.where(ahead[None], near[:, None, :], 0), axis=2)
    near_count = jnp.sum(near, axis=1, keepdims=True)
    place = jnp.where(near == 1, near_ahead, near_count + order[None, :] - near_ahead)
    hit = place[:, None, :] == order[None, :, None]
    table = jnp.sum(jnp.where(hit, slot[:, None, :], 0), axis=2).reshape(-1)
    early = jnp.min(near_count.reshape(blocks // 2, 2), axis=1) // 2
    early = jnp.minimum(early, MOST_EARLY)
    live = lax.dynamic_slice_in_dim(counts, rank, 1, 0)

    kept = (
        ((blocks, LANES, LANES), bf16),
        ((blocks, 3, 32, LANES), bf16),
        ((blocks, 3, LANES, LANES), bf16),
        ((blocks, 3, 8, LANES), f32),
    )
    near_results = pl.pallas_call(
        near_kernel,
        out_shape=tuple(pltpu.HBM(*k) for k in kept),
        in_specs=[smem(), smem(), hbm(), hbm()],
        out_specs=(hbm(),) * 4,
        scratch_shapes=[pltpu.VMEM(*k) for k in kept]
        + [
            pltpu.VMEM((9, blocks, LANES), f32),
            pltpu.VMEM((3, blocks * LANES), f32),
            pltpu.SemaphoreType.DMA((4,)),
        ],
        compiler_params=pltpu.CompilerParams(vmem_limit_bytes=16 << 20),
        cost_estimate=pl.CostEstimate(
            flops=10_000_000_000, bytes_accessed=6_000_000, transcendentals=0
        ),
        name="near_rates",
    )(table, early, nodes, strengths)

    slots = blocks + 2 * groups
    base, step = pl.pallas_call(
        rest_kernel,
        out_shape=(
            pltpu.HBM((9, blocks, LANES), f32),
            jax.ShapeDtypeStruct((3, blocks, LANES), f32),
        ),
        in_specs=[smem()] * 3 + [vmem()] + [hbm()] * 6,
        out_specs=(hbm(), vmem()),
        scratch_shapes=[
            pltpu.VMEM((slots, LANES, LANES), bf16),
            pltpu.VMEM((slots, 3, 32, LANES), bf16),
            pltpu.VMEM(*kept[2]),
            pltpu.VMEM(*kept[3]),
            pltpu.VMEM((9, blocks, LANES), f32),
            pltpu.VMEM((3, blocks * LANES), f32),
            pltpu.VMEM((9, blocks, LANES), f32),
            pltpu.SemaphoreType.DMA((6,)),
        ],
        compiler_params=pltpu.CompilerParams(vmem_limit_bytes=24 << 20),
        name="rest_rates",
    )(table, early, live, far, *map(in_hbm, near_results), nodes, start_state)

    return add_earlier(base, step, slices).reshape(1, 9, blocks * LANES)


def solution(mesh):
    return jax.shard_map(
        shards,
        mesh=mesh,
        in_specs=(P("tm", None, "space"), P(None, "space"), P(None, "space"), P(), P()),
        out_specs=P("tm", None, "space"),
        check_vma=False,
    )
```

time: 92.8 us -> 74.2 us (0.80)
  the two profiles are of different devices: /device:TPU:16 before, /device:TPU:1 now
where the time goes in v2:
time: 74.2 us; the launch traced here: 73.3 us
  Pallas kernels  46.8 us (63%)
  starting transfers between devices  16.4 us (22%)
  waiting for transfers between devices  4.65 us (6%)
  local copies, waits for them, and re-layouts  2.81 us (4%)
  other arithmetic  2.5 us (3%)
    pallas_call x1, Pallas kernels, shards(): pl.pallas_call(rest_kernel, out_shape=(pltpu.HBM((9, blocks, LANES), f32)...  27.5 us
    pallas_call x1, Pallas kernels, shards(): pl.pallas_call(near_kernel, out_shape=tuple((pltpu.HBM(*k) for k in kept)...  15.1 us
    all_to_all x1, starting transfers between devices, shards(): far = lax.all_to_all(send, 'space', 0, 0, tiled=True)  11.9 us
    ppermute x4, waiting for transfers between devices, swap(): return lax.ppermute(value, 'tm', [(i, i ^ k) for i in range(slices)])  4.65 us
    ppermute x4, starting transfers between devices, swap(): return lax.ppermute(value, 'tm', [(i, i ^ k) for i in range(slices)])  4.52 us
    pallas_call x1, Pallas kernels, shards(): pl.pallas_call(gather_kernel, out_shape=jax.ShapeDtypeStruct((groups, 24,...  2.61 us
    pallas_call x1, Pallas kernels, add_earlier(): pl.pallas_call(functools.partial(sum_kernel, shifts), out_shape=jax.Shape...  1.59 us
  transfers between devices with their start and end apart: 5, of which 3 were waited for; matrix products, arithmetic and copies ran while one was open for 5% of the time, Pallas kernels for 21%

profile of v2, /device:TPU:1, one launch (start us, length us, event | category | flops | bytes accessed | tf_op | source)
XLA Modules:
  0.0 73.3 jit_solution(1494839111149955255)
XLA Ops:
  0.0 0.9 %select_reduce_fusion.3 = (s32[1024]{0:T(1024)S(1)}, s32[1024]{0:T(1024)S(1)}) fusion(s32[1024,12]{0,1:T(8,128)} %param.8, s32[]{:T(128)S(6)} %axis_index.12), kind=kLoop, calls=%fused_computation.10 | loop fusion | flops 292864 | bytes 57348 | tf_op jit(solution)/shard_map/reduce_min | solution.py:372
  0.9 0.1 reduce_min.37
  1.0 0.1 reduce_max.14
  1.1 0.1 reduce_min.38
  1.2 0.1 reduce_max.18
  1.3 2.6 %gather_blocks.1 = f32[32,24,128]{2,1,0:T(8,128)} custom-call(s32[2,32]{1,0:T(2,128)S(1)} %pad_add_fusion.pick_ref, f32[9,32,128]{2,1,0:T(8,128)} %bitcast.4, f32[3,4096]{1,0:T(4,128)} %strength_in.3), custom_call_target="tpu_custom_call" | custom-call | tf_op jit(solution)/shard_map/gather_blocks/pallas_call | solution.py:374
  4.0 11.9 %all-to-all-start = ((f32[32,24,128]{2,1,0:T(8,128)}), f32[32,24,128]{2,1,0:T(8,128)S(1)}, u32[]{:S(2)}, u32[]{:S(2)}) async-start(f32[32,24,128]{2,1,0:T(8,128)} %gather_blocks.1), calls=%async_computation | async-start | bytes 786432 | tf_op jit(solution)/shard_map/all_to_all | solution.py:387
  15.8 0.8 %constant_dynamic-slice_fusion = s32[32,12]{0,1:T(8,128)S(1)} fusion(s32[1024,12]{0,1:T(8,128)} %param.8, s32[]{:T(128)S(6)} %select_n.85), kind=kLoop, calls=%fused_computation.42 | loop fusion | bytes 3076 | tf_op jit(solution)/shard_map/dynamic_slice | solution.py:389
  16.6 0.1 copy.12
  16.7 0.1 reshape.121
  16.8 0.1 select_reduce_fusion.5
  17.0 0.1 select_reduce_fusion.4
  17.1 0.1 reduce_sum.39
  17.2 0.1 copy.13
  17.2 0.8 %fusion.6 = (s32[32]{0:T(128)S(1)}, s32[32,12]{0,1:T(8,128)S(1)}) fusion(s32[32,12]{0,1:T(8,128)S(1)} %copy.13, s32[]{:T(128)S(6)} %axis_index.12, s32[1024,12]{0,1:T(8,128)} %param.8, s32[]{:T(128)S(6)} %select_n.85), kind=kLoop, calls=%fused_computation.43 | loop fusion | flops 11104 | bytes 4744 | tf_op jit(solution)/shard_map/reduce_sum | solution.py:401
  18.0 0.1 reshape_broadcast_in_dim.3
  18.1 0.1 reduce_min.35
  18.3 0.1 select_reduce_fusion.1
  18.5 0.1 copy.14
  18.5 0.1 reshape.122.table_ref
  18.6 1.2 %dynamic_slice.7.live_ref = s32[1]{0:T(128)} dynamic-slice(s32[32]{0:T(128)} %param.9, s32[]{:T(128)S(6)} %select_n.97), dynamic_slice_sizes={1} | dynamic-slice | bytes 12 | tf_op jit(solution)/shard_map/dynamic_slice | solution.py:407
  19.9 15.1 %near_rates.1 = (bf16[32,128,128]{2,1,0:T(8,128)(2,1)}, bf16[32,3,32,128]{3,2,1,0:T(8,128)(2,1)}, bf16[32,3,128,128]{3,2,1,0:T(8,128)(2,1)}, f32[32,3,8,128]{3,2,1,0:T(8,128)}) custom-call(s32[384]{0:T(512)S(1)} %reshape.122.table_ref, s32[16]{0:T(128)S(1)} %fusion.5.early_ref, f32[9,32,128]{2,1,0:T(8,128)} %bitcast.5, f32[3,4096]{1,0:T(4,128)} %strength_in.3), custom_call_target="tpu_custom_call" | custom-call | flops 10000000000 | bytes 6000000 | tf_op jit(solution)/shard_map/near_rates/pallas_call | solution.py:415
  35.0 0.0 all-to-all-done.far_ref
  35.0 27.5 %rest_rates.1 = (f32[9,32,128]{2,1,0:T(8,128)}, f32[3,32,128]{2,1,0:T(8,128)S(1)}) custom-call(s32[384]{0:T(512)S(1)} %reshape.122.table_ref, s32[16]{0:T(128)S(1)} %fusion.5.early_ref, s32[1]{0:T(128)} %dynamic_slice.7.live_ref, f32[32,24,128]{2,1,0:T(8,128)S(1)} %all-to-all-done.far_ref, bf16[32,128,128]{2,1,0:T(8,128)(2,1)} %get-tuple-element.11.near_feature, ...), custom_call_target="tpu_custom_call" | custom-call | tf_op jit(solution)/shard_map/rest_rates/pallas_call | solution.py:434
  62.5 1.0 %collective-permute-start = (f32[3,32,128]{2,1,0:T(8,128)S(1)}, f32[3,32,128]{2,1,0:T(8,128)S(1)}, u32[]{:S(2)}, u32[]{:S(2)}) collective-permute-start(f32[3,32,128]{2,1,0:T(8,128)S(1)} %get-tuple-element.16), channel_id=1, source_target_pairs={{0,32},{32,0},{64,96},{96,64},{128,160},{160,128},{192,224},{224,1... | collective-permute-start | bytes 147464 | tf_op jit(solution)/shard_map/ppermute | solution.py:344
  63.5 0.9 %collective-permute-done.other_ref = f32[3,32,128]{2,1,0:T(8,128)S(1)} collective-permute-done((f32[3,32,128]{2,1,0:T(8,128)S(1)}, f32[3,32,128]{2,1,0:T(8,128)S(1)}, u32[]{:S(2)}, u32[]{:S(2)}) %collective-permute-start) | collective-permute-done | bytes 49184 | tf_op jit(solution)/shard_map/ppermute | solution.py:344
  64.4 2.8 %collective-permute-start.3 = (f32[3,32,128]{2,1,0:T(8,128)S(1)}, f32[3,32,128]{2,1,0:T(8,128)S(1)}, u32[]{:S(2)}, u32[]{:S(2)}) collective-permute-start(f32[3,32,128]{2,1,0:T(8,128)S(1)} %add.76), channel_id=1, source_target_pairs={{0,192},{32,224},{64,128},{96,160},{128,64},{160,96},{192,0},{224,... | collective-permute-start | bytes 147464 | tf_op jit(solution)/shard_map/ppermute | solution.py:344
  67.2 0.3 collective-permute-start.2
  67.6 0.3 collective-permute-start.1
  67.9 0.8 %collective-permute-done.3.refs_2_ = f32[3,32,128]{2,1,0:T(8,128)S(1)} collective-permute-done((f32[3,32,128]{2,1,0:T(8,128)S(1)}, f32[3,32,128]{2,1,0:T(8,128)S(1)}, u32[]{:S(2)}, u32[]{:S(2)}) %collective-permute-start.3) | collective-permute-done | bytes 49184 | tf_op jit(solution)/shard_map/ppermute | solution.py:344
  68.7 3.0 %collective-permute-done.2.refs_1_ = f32[3,32,128]{2,1,0:T(8,128)S(1)} collective-permute-done((f32[3,32,128]{2,1,0:T(8,128)S(1)}, f32[3,32,128]{2,1,0:T(8,128)S(1)}, u32[]{:S(2)}, u32[]{:S(2)}) %collective-permute-start.2) | collective-permute-done | bytes 49184 | tf_op jit(solution)/shard_map/ppermute | solution.py:344
  71.7 0.0 collective-permute-done.1.refs_0_
  71.7 1.6 %add_earlier.1 = f32[9,32,128]{2,1,0:T(8,128)} custom-call(f32[9,32,128]{2,1,0:T(8,128)} %get-tuple-element.15.base_in, f32[3,32,128]{2,1,0:T(8,128)S(1)} %collective-permute-done.other_ref, f32[3,32,128]{2,1,0:T(8,128)S(1)} %collective-permute-done.1.refs_0_, f32[3,32,128]{2,1,0:T(8,128)S(1)} %collective-permute-done.2.refs_1_, ...), custom_call_target="tpu_custom_call" | custom-call | tf_op jit(solution)/shard_map/add_earlier/pallas_call | solution.py:350
  (8 shorter events, 0.1 us)
Async XLA Ops:
  4.0 31.0 %all-to-all-start = ((f32[32,24,128]{2,1,0:T(8,128)}), f32[32,24,128]{2,1,0:T(8,128)S(1)}, u32[]{:S(2)}, u32[]{:S(2)}) async-start(f32[32,24,128]{2,1,0:T(8,128)} %gather_blocks.1), calls=%async_computation | async-start | bytes 786432 | tf_op jit(solution)/shard_map/all_to_all | solution.py:387
  62.5 1.9 %collective-permute-start = (f32[3,32,128]{2,1,0:T(8,128)S(1)}, f32[3,32,128]{2,1,0:T(8,128)S(1)}, u32[]{:S(2)}, u32[]{:S(2)}) collective-permute-start(f32[3,32,128]{2,1,0:T(8,128)S(1)} %get-tuple-element.16), channel_id=1, source_target_pairs={{0,32},{32,0},{64,96},{96,64},{128,160},{160,128},{192,224},{224,1... | collective-permute-start | bytes 147464 | tf_op jit(solution)/shard_map/ppermute | solution.py:344
  64.4 4.3 %collective-permute-start.3 = (f32[3,32,128]{2,1,0:T(8,128)S(1)}, f32[3,32,128]{2,1,0:T(8,128)S(1)}, u32[]{:S(2)}, u32[]{:S(2)}) collective-permute-start(f32[3,32,128]{2,1,0:T(8,128)S(1)} %add.76), channel_id=1, source_target_pairs={{0,192},{32,224},{64,128},{96,160},{128,64},{160,96},{192,0},{224,... | collective-permute-start | bytes 147464 | tf_op jit(solution)/shard_map/ppermute | solution.py:344
  67.2 4.4 %collective-permute-start.2 = (f32[3,32,128]{2,1,0:T(8,128)S(1)}, f32[3,32,128]{2,1,0:T(8,128)S(1)}, u32[]{:S(2)}, u32[]{:S(2)}) collective-permute-start(f32[3,32,128]{2,1,0:T(8,128)S(1)} %add.76), channel_id=1, source_target_pairs={{0,128},{32,160},{64,192},{96,224},{128,0},{160,32},{192,64},{224,... | collective-permute-start | bytes 147464 | tf_op jit(solution)/shard_map/ppermute | solution.py:344
  67.6 4.1 %collective-permute-start.1 = (f32[3,32,128]{2,1,0:T(8,128)S(1)}, f32[3,32,128]{2,1,0:T(8,128)S(1)}, u32[]{:S(2)}, u32[]{:S(2)}) collective-permute-start(f32[3,32,128]{2,1,0:T(8,128)S(1)} %add.76), channel_id=1, source_target_pairs={{0,64},{32,96},{64,0},{96,32},{128,192},{160,224},{192,128},{224,1... | collective-permute-start | bytes 147464 | tf_op jit(solution)/shard_map/ppermute | solution.py:344

commit v3 on v2

--- a/solution.py
+++ b/solution.py
@@ -13,7 +13,9 @@
 step_size = 1.0
 LANES = 128
 ROWS = 16
-MOST_EARLY = 3
+LIST = 12
+TOGETHER = 4
+MOST_EARLY = 2
 bf16 = jnp.bfloat16
 f32 = jnp.float32
 
@@ -71,13 +73,30 @@
     ones = jnp.ones((ROWS, LANES), bf16)
     stacked = jnp.concatenate([first, second, first, second, third, first, norms, ones], 0)
     feature_ref[slot] = stacked.T
-    strength = [rows[9 + c : 10 + c] for c in range(3)]
-    blank = jnp.zeros((2, LANES), f32)
+    place = lax.broadcasted_iota(jnp.int32, (ROWS, LANES), 0)
+
+    def turned(value):
+        ahead = jnp.where(place % 3 == 2, pltpu.roll(value, 2, 0), pltpu.roll(value, ROWS - 1, 0))
+        behind = jnp.where(place % 3 == 0, pltpu.roll(value, ROWS - 2, 0), pltpu.roll(value, 1, 0))
+        return ahead, behind
+
+    strength = jnp.where(
+        place < 3,
+        pltpu.roll(rows, ROWS - 9, 0),
+        jnp.where(place < 6, pltpu.roll(rows, ROWS - 6, 0), pltpu.roll(rows, ROWS - 3, 0)),
+    )
+    ahead, behind = turned(rows)
+    strength_ahead, strength_behind = turned(strength)
+    weights = jnp.where(place < 9, ahead * strength_behind - behind * strength_ahead, rows)
+    parts = [piece.astype(f32) for piece in pieces(weights)]
+    top = place < 3
+    blank = jnp.zeros((8, LANES), f32)
     for m in range(3):
-        place = [rows[3 * m + c : 3 * m + c + 1] for c in range(3)]
-        weights = jnp.concatenate(strength + cross(place, strength) + [blank], 0)
-        parts = [piece.astype(f32) for piece in pieces(weights)]
-        weight_ref[slot, m] = jnp.concatenate(parts + [jnp.zeros((8, LANES), f32)], 0).astype(bf16)
+        made = [
+            jnp.where(top, pltpu.roll(p, (ROWS - 3 * m) % ROWS, 0), pltpu.roll(p, ROWS - 6, 0))[0:8]
+            for p in parts
+        ]
+        weight_ref[slot, m] = jnp.concatenate(made + [blank], 0).astype(bf16)
 
 
 def target_features(rows, target_ref, t):
@@ -97,9 +116,8 @@
     return pl.ds(pl.multiple_of(t * LANES, LANES), LANES)
 
 
-def pair_sums(table_ref, target_ref, feature_ref, weight_ref, i, m, begin, end):
-    list_len = table_ref.shape[0] // target_ref.shape[0]
-    ids = (2 * i, 2 * i + 1)
+def pair_sums(table_ref, target_ref, feature_ref, weight_ref, ids, m, begin, end):
+    list_len = LIST
     zero = jnp.zeros((LANES, LANES), bf16)
     both = jnp.concatenate(
         [
@@ -142,6 +160,12 @@
     return copies
 
 
+def group_pairs(table_ref, early, blocks, i):
+    first = early + blocks // (2 * TOGETHER) + 2 * TOGETHER * i
+    ids = [table_ref[first + k] for k in range(2 * TOGETHER)]
+    return [(ids[2 * k], ids[2 * k + 1]) for k in range(TOGETHER)]
+
+
 def gather_kernel(pick_ref, node_in, strength_in, send_ref, node_ref, strength_ref, sems):
     for copy in fetch(((node_in, node_ref), (strength_in, strength_ref)), sems):
         copy.wait()
@@ -158,7 +182,6 @@
 
 def near_kernel(
     table_ref,
-    early_ref,
     node_in,
     strength_in,
     feature_out,
@@ -174,6 +197,7 @@
     sems,
 ):
     blocks = part_ref.shape[0]
+    early = LIST * blocks
     for copy in fetch(((node_in, node_ref), (strength_in, strength_ref)), sems):
         copy.wait()
 
@@ -190,21 +214,24 @@
     kept = ((feature_ref, feature_out), (weight_ref, weight_out), (target_ref, target_out))
     copies = fetch(kept, sems)
 
-    def pair(i, _):
+    def group(i, _):
         for steps in range(MOST_EARLY + 1):
 
-            @pl.when(early_ref[i] == steps)
+            @pl.when(table_ref[early + i] == steps)
             def _():
-                for m in range(3):
-                    sums = pair_sums(
-                        table_ref, target_ref, feature_ref, weight_ref, i, m, 0, 2 * steps
-                    )
-                    for q in range(2):
-                        part_ref[2 * i + q, m] = sums[q]
-
-        return 0
-
-    lax.fori_loop(0, blocks // 2, pair, 0)
+                made = []
+                for ids in group_pairs(table_ref, early, blocks, i):
+                    for m in range(3):
+                        sums = pair_sums(
+                            table_ref, target_ref, feature_ref, weight_ref, ids, m, 0, 2 * steps
+                        )
+                        made.extend((t, m, value) for t, value in zip(ids, sums))
+                for t, m, value in made:
+                    part_ref[t, m] = value
+
+        return 0
+
+    lax.fori_loop(0, blocks // (2 * TOGETHER), group, 0)
     copies.append(pltpu.make_async_copy(part_ref, part_out, sems.at[3]))
     copies[3].start()
     for copy in copies:
@@ -213,8 +240,7 @@
 
 def rest_kernel(
     table_ref,
-    early_ref,
-    live_ref,
+    count_ref,
     far_ref,
     near_feature,
     near_weight,
@@ -234,7 +260,7 @@
     sems,
 ):
     blocks = part_ref.shape[0]
-    list_len = table_ref.shape[0] // blocks
+    early = LIST * blocks
     radau = radau_matrix() * step_size
 
     def far_source(i, _):
@@ -256,55 +282,47 @@
     lax.fori_loop(0, far_ref.shape[0], far_source, 0, unroll=2)
     for copy in copies:
         copy.wait()
-    live = live_ref[0]
-
-    def pair(i, _):
+    live = count_ref[lax.axis_index("space")]
+
+    def group(i, _):
         for steps in range(MOST_EARLY + 1):
 
-            @pl.when(early_ref[i] == steps)
+            @pl.when(table_ref[early + i] == steps)
             def _():
-                finish(i, 2 * steps)
-
-        return 0
-
-    def finish(i, begin):
-        lanes = [lanes_of(2 * i + q) for q in range(2)]
-        rows = [node_ref[:, 2 * i + q, :] for q in range(2)]
-        velocity = ([], [])
+                made = []
+                for ids in group_pairs(table_ref, early, blocks, i):
+                    for m in range(3):
+                        sums = pair_sums(
+                            table_ref, target_ref, feature_ref, weight_ref, ids, m, 2 * steps, LIST
+                        )
+                        made.extend((t, m, value) for t, value in zip(ids, sums))
+                for t, m, value in made:
+                    part_ref[t, m] = part_ref[t, m] + value
+
+        return 0
+
+    def close(t, _):
+        rows = node_ref[:, t, :]
+        start = start_ref[:, lanes_of(t)]
+        on = jnp.where(t < live, 1.0, 0.0).astype(f32)
+        velocity = []
         for m in range(3):
-            both = pair_sums(
-                table_ref, target_ref, feature_ref, weight_ref, i, m, begin, list_len
-            )
-            for q in range(2):
-                sums = both[q] + part_ref[2 * i + q, m]
-                place = [rows[q][3 * m + c : 3 * m + c + 1] for c in range(3)]
-                spread = cross(place, [sums[c : c + 1] for c in range(3)])
-                velocity[q].append(
-                    [(spread[c] - sums[3 + c : 4 + c]) * (-0.25 / math.pi) for c in range(3)]
-                )
-        for q in range(2):
-            on = jnp.where(2 * i + q < live, 1.0, 0.0).astype(f32)
-            start = start_ref[:, lanes[q]]
-            for k in range(3):
-                step = [
-                    sum(float(radau[k, n]) * velocity[q][n][c] for n in range(3)) * on
-                    for c in range(3)
-                ]
-                for c in range(3):
-                    base_ref[3 * k + c, pl.ds(2 * i + q, 1), :] = start[c : c + 1] + step[c]
-                    if k == 2:
-                        step_ref[c, pl.ds(2 * i + q, 1), :] = step[c]
-
-    half = blocks // 2
-    copies = []
-    for k in range(2):
-        lax.fori_loop(k * half // 2, (k + 1) * half // 2, pair, 0)
-        rows = pl.ds(k * half, half)
-        copy = pltpu.make_async_copy(base_ref.at[:, rows], base_out.at[:, rows], sems.at[k])
-        copy.start()
-        copies.append(copy)
-    for copy in copies:
-        copy.wait()
+            sums = part_ref[t, m]
+            place = [rows[3 * m + c : 3 * m + c + 1] for c in range(3)]
+            spread = cross(place, [sums[3 + c : 4 + c] for c in range(3)])
+            velocity.append([(spread[c] - sums[c : c + 1]) * (-0.25 / math.pi) for c in range(3)])
+        for k in range(3):
+            for c in range(3):
+                step = sum(float(radau[k, n]) * velocity[n][c] for n in range(3)) * on
+                base_ref[3 * k + c, pl.ds(t, 1), :] = start[c : c + 1] + step
+                if k == 2:
+                    step_ref[c, pl.ds(t, 1), :] = step
+        return 0
+
+    lax.fori_loop(0, blocks // (2 * TOGETHER), group, 0)
+    lax.fori_loop(0, blocks, close, 0, unroll=4)
+    (copy,) = fetch(((base_ref, base_out),), sems)
+    copy.wait()
 
 
 def hbm():
@@ -402,9 +420,15 @@
     place = jnp.where(near == 1, near_ahead, near_count + order[None, :] - near_ahead)
     hit = place[:, None, :] == order[None, :, None]
     table = jnp.sum(jnp.where(hit, slot[:, None, :], 0), axis=2).reshape(-1)
-    early = jnp.min(near_count.reshape(blocks // 2, 2), axis=1) // 2
-    early = jnp.minimum(early, MOST_EARLY)
-    live = lax.dynamic_slice_in_dim(counts, rank, 1, 0)
+    count, number = near_count[:, 0], jnp.arange(blocks, dtype=jnp.int32)
+    before = (count[None, :] > count[:, None]) | (
+        (count[None, :] == count[:, None]) & (number[None, :] < number[:, None])
+    )
+    at = jnp.sum(before.astype(jnp.int32), axis=1)
+    sorted_targets = jnp.sum(jnp.where(at[None, :] == number[:, None], number[None, :], 0), axis=1)
+    last = jnp.arange(2 * TOGETHER - 1, blocks, 2 * TOGETHER, dtype=jnp.int32)
+    early = jnp.sum(jnp.where(at[None, :] == last[:, None], count[None, :] // 2, 0), axis=1)
+    table = jnp.concatenate([table, jnp.minimum(early, MOST_EARLY), sorted_targets])
 
     kept = (
         ((blocks, LANES, LANES), bf16),
@@ -415,7 +439,7 @@
     near_results = pl.pallas_call(
         near_kernel,
         out_shape=tuple(pltpu.HBM(*k) for k in kept),
-        in_specs=[smem(), smem(), hbm(), hbm()],
+        in_specs=[smem(), hbm(), hbm()],
         out_specs=(hbm(),) * 4,
         scratch_shapes=[pltpu.VMEM(*k) for k in kept]
         + [
@@ -428,7 +452,7 @@
             flops=10_000_000_000, bytes_accessed=6_000_000, transcendentals=0
         ),
         name="near_rates",
-    )(table, early, nodes, strengths)
+    )(table, nodes, strengths)
 
     slots = blocks + 2 * groups
     base, step = pl.pallas_call(
@@ -437,7 +461,7 @@
             pltpu.HBM((9, blocks, LANES), f32),
             jax.ShapeDtypeStruct((3, blocks, LANES), f32),
         ),
-        in_specs=[smem()] * 3 + [vmem()] + [hbm()] * 6,
+        in_specs=[smem()] * 2 + [vmem()] + [hbm()] * 6,
         out_specs=(hbm(), vmem()),
         scratch_shapes=[
             pltpu.VMEM((slots, LANES, LANES), bf16),
@@ -451,7 +475,7 @@
         ],
         compiler_params=pltpu.CompilerParams(vmem_limit_bytes=24 << 20),
         name="rest_rates",
-    )(table, early, live, far, *map(in_hbm, near_results), nodes, start_state)
+    )(table, counts, far, *map(in_hbm, near_results), nodes, start_state)
 
     return add_earlier(base, step, slices).reshape(1, 9, blocks * LANES)
 

time: 74.2 us -> 67.3 us (0.907)
  Pallas kernels: 46.8 us -> 38.2 us
  starting transfers between devices: 16.4 us -> 17.9 us
  local copies, waits for them, and re-layouts: 2.81 us -> 1.49 us
  waiting for transfers between devices: 4.65 us -> 5.6 us
    pallas_call x1, Pallas kernels: 15.1 us -> 9.67 us  [shards(): pl.pallas_call(near_kernel, out_shape=tuple((pltpu.HBM(*k) for k in kept)...]
    pallas_call x1, Pallas kernels: 27.5 us -> 24.3 us  [shards(): pl.pallas_call(rest_kernel, out_shape=(pltpu.HBM((9, blocks, LANES), f32)...]
    ppermute x4, starting transfers between devices: 4.52 us -> 6.07 us  [swap(): return lax.ppermute(value, 'tm', [(i, i ^ k) for i in range(slices)])]
    dynamic_slice x1 -> x0, local copies, waits for them, and re-layouts: 1.24 us -> none  [shards(): live = lax.dynamic_slice_in_dim(counts, rank, 1, 0)]
    all_to_all x1, waiting for transfers between devices: 0.01 us -> 0.95 us  [shards(): far = lax.all_to_all(send, 'space', 0, 0, tiled=True)]
    convert_element_type x1, other arithmetic: 0.01 us -> 0.79 us  [shards(): near = (slot < blocks).astype(jnp.int32)]
    reduce_sum x1, other arithmetic: 0.81 us -> 0.02 us  [shards(): near_count = jnp.sum(near, axis=1, keepdims=True)]
  transfers between devices with their start and end apart: 5 -> 5, of which waited for: 3 -> 4; matrix products, arithmetic and copies ran while one was open for 5% -> 5% of each run, Pallas kernels for 21% -> 15%
where the time goes in v3:
time: 67.3 us; the launch traced here: 66.5 us
  Pallas kernels  38.2 us (57%)
  starting transfers between devices  17.9 us (27%)
  waiting for transfers between devices  5.6 us (8%)
  other arithmetic  2.94 us (4%)
  local copies, waits for them, and re-layouts  1.49 us (2%)
    pallas_call x1, Pallas kernels, shards(): pl.pallas_call(rest_kernel, out_shape=(pltpu.HBM((9, blocks, LANES), f32)...  24.3 us
    all_to_all x1, starting transfers between devices, shards(): far = lax.all_to_all(send, 'space', 0, 0, tiled=True)  11.9 us
    pallas_call x1, Pallas kernels, shards(): pl.pallas_call(near_kernel, out_shape=tuple((pltpu.HBM(*k) for k in kept)...  9.67 us
    ppermute x4, starting transfers between devices, swap(): return lax.ppermute(value, 'tm', [(i, i ^ k) for i in range(slices)])  6.07 us
    ppermute x4, waiting for transfers between devices, swap(): return lax.ppermute(value, 'tm', [(i, i ^ k) for i in range(slices)])  4.65 us
    pallas_call x1, Pallas kernels, shards(): pl.pallas_call(gather_kernel, out_shape=jax.ShapeDtypeStruct((groups, 24,...  2.61 us
    pallas_call x1, Pallas kernels, add_earlier(): pl.pallas_call(functools.partial(sum_kernel, shifts), out_shape=jax.Shape...  1.59 us
  transfers between devices with their start and end apart: 5, of which 4 were waited for; matrix products, arithmetic and copies ran while one was open for 5% of the time, Pallas kernels for 15%

profile of v3, /device:TPU:1, one launch (start us, length us, event | category | flops | bytes accessed | tf_op | source)
XLA Modules:
  0.0 66.5 jit_solution(7404097718460410274)
XLA Ops:
  0.0 0.9 %select_reduce_fusion.3 = (s32[1024]{0:T(1024)S(1)}, s32[1024]{0:T(1024)S(1)}) fusion(s32[1024,12]{0,1:T(8,128)} %param.8, s32[]{:T(128)S(6)} %axis_index.12), kind=kLoop, calls=%fused_computation.10 | loop fusion | flops 292864 | bytes 57348 | tf_op jit(solution)/shard_map/reduce_min | solution.py:390
  0.9 0.1 reduce_min.27
  1.0 0.1 reduce_max.14
  1.1 0.1 reduce_min.28
  1.2 0.1 reduce_max.18
  1.3 2.6 %gather_blocks.1 = f32[32,24,128]{2,1,0:T(8,128)} custom-call(s32[2,32]{1,0:T(2,128)S(1)} %pad_add_fusion.1.pick_ref, f32[9,32,128]{2,1,0:T(8,128)} %bitcast.4, f32[3,4096]{1,0:T(4,128)} %strength_in.3), custom_call_target="tpu_custom_call" | custom-call | tf_op jit(solution)/shard_map/gather_blocks/pallas_call | solution.py:392
  4.0 11.9 %all-to-all-start = ((f32[32,24,128]{2,1,0:T(8,128)}), f32[32,24,128]{2,1,0:T(8,128)S(1)}, u32[]{:S(2)}, u32[]{:S(2)}) async-start(f32[32,24,128]{2,1,0:T(8,128)} %gather_blocks.1), calls=%async_computation | async-start | bytes 786432 | tf_op jit(solution)/shard_map/all_to_all | solution.py:405
  15.9 0.8 %constant_dynamic-slice_fusion = s32[32,12]{0,1:T(8,128)S(1)} fusion(s32[1024,12]{0,1:T(8,128)} %param.8, s32[]{:T(128)S(6)} %select_n.95), kind=kLoop, calls=%fused_computation.51 | loop fusion | bytes 3076 | tf_op jit(solution)/shard_map/dynamic_slice | solution.py:407
  16.6 0.1 copy.12
  16.7 0.1 reshape.163
  16.8 0.1 select_reduce_fusion.5
  17.0 0.1 select_reduce_fusion.4
  17.1 0.1 reduce_sum.66
  17.2 0.1 copy.13
  17.2 0.8 %compare_convert_fusion = (s32[32,12]{0,1:T(8,128)S(1)}, s32[32,12]{0,1:T(8,128)S(1)}) fusion(s32[32,12]{0,1:T(8,128)S(1)} %copy.13, s32[]{:T(128)S(6)} %axis_index.12, s32[1024,12]{0,1:T(8,128)} %param.8, s32[]{:T(128)S(6)} %select_n.95), kind=kLoop, calls=%fused_computation.33 | loop fusion | flops 10752 | bytes 6152 | tf_op jit(solution)/shard_map/convert_element_type | solution.py:415
  18.1 0.2 convert_reduce_fusion
  18.3 0.1 select_reduce_fusion.1
  18.4 0.1 select_reduce_fusion.6
  18.5 0.2 select_reduce_fusion.7
  18.7 0.1 copy.14
  18.8 0.1 reshape.164
  18.9 0.1 pad_add_fusion.table_ref
  19.0 0.0 copy-start
  19.0 9.7 %near_rates.1 = (bf16[32,128,128]{2,1,0:T(8,128)(2,1)}, bf16[32,3,32,128]{3,2,1,0:T(8,128)(2,1)}, bf16[32,3,128,128]{3,2,1,0:T(8,128)(2,1)}, f32[32,3,8,128]{3,2,1,0:T(8,128)}) custom-call(s32[420]{0:T(512)S(1)} %pad_add_fusion.table_ref, f32[9,32,128]{2,1,0:T(8,128)} %bitcast.5, f32[3,4096]{1,0:T(4,128)} %strength_in.3), custom_call_target="tpu_custom_call" | custom-call | flops 10000000000 | bytes 6000000 | tf_op jit(solution)/shard_map/near_rates/pallas_call | solution.py:439
  28.7 1.0 %all-to-all-done.far_ref = f32[32,24,128]{2,1,0:T(8,128)S(1)} async-done(((f32[32,24,128]{2,1,0:T(8,128)}), f32[32,24,128]{2,1,0:T(8,128)S(1)}, u32[]{:S(2)}, u32[]{:S(2)}) %all-to-all-start) | async-done | bytes 393248 | tf_op jit(solution)/shard_map/all_to_all | solution.py:405
  29.6 0.0 copy-done
  29.6 24.3 %rest_rates.1 = (f32[9,32,128]{2,1,0:T(8,128)}, f32[3,32,128]{2,1,0:T(8,128)S(1)}) custom-call(s32[420]{0:T(512)S(1)} %pad_add_fusion.table_ref, s32[32]{0:T(128)S(1)} %copy-done, f32[32,24,128]{2,1,0:T(8,128)S(1)} %all-to-all-done.far_ref, bf16[32,128,128]{2,1,0:T(8,128)(2,1)} %get-tuple-element.11.near_feature, ...), custom_call_target="tpu_custom_call" | custom-call | tf_op jit(solution)/shard_map/rest_rates/pallas_call | solution.py:458
  54.0 2.6 %collective-permute-start = (f32[3,32,128]{2,1,0:T(8,128)S(1)}, f32[3,32,128]{2,1,0:T(8,128)S(1)}, u32[]{:S(2)}, u32[]{:S(2)}) collective-permute-start(f32[3,32,128]{2,1,0:T(8,128)S(1)} %get-tuple-element.16), channel_id=1, source_target_pairs={{0,32},{32,0},{64,96},{96,64},{128,160},{160,128},{192,224},{224,1... | collective-permute-start | bytes 147464 | tf_op jit(solution)/shard_map/ppermute | solution.py:362
  56.6 0.9 %collective-permute-done.other_ref = f32[3,32,128]{2,1,0:T(8,128)S(1)} collective-permute-done((f32[3,32,128]{2,1,0:T(8,128)S(1)}, f32[3,32,128]{2,1,0:T(8,128)S(1)}, u32[]{:S(2)}, u32[]{:S(2)}) %collective-permute-start) | collective-permute-done | bytes 49184 | tf_op jit(solution)/shard_map/ppermute | solution.py:362
  57.4 2.8 %collective-permute-start.3 = (f32[3,32,128]{2,1,0:T(8,128)S(1)}, f32[3,32,128]{2,1,0:T(8,128)S(1)}, u32[]{:S(2)}, u32[]{:S(2)}) collective-permute-start(f32[3,32,128]{2,1,0:T(8,128)S(1)} %add.85), channel_id=1, source_target_pairs={{0,192},{32,224},{64,128},{96,160},{128,64},{160,96},{192,0},{224,... | collective-permute-start | bytes 147464 | tf_op jit(solution)/shard_map/ppermute | solution.py:362
  60.3 0.3 collective-permute-start.2
  60.6 0.3 collective-permute-start.1
  60.9 0.8 %collective-permute-done.3.refs_2_ = f32[3,32,128]{2,1,0:T(8,128)S(1)} collective-permute-done((f32[3,32,128]{2,1,0:T(8,128)S(1)}, f32[3,32,128]{2,1,0:T(8,128)S(1)}, u32[]{:S(2)}, u32[]{:S(2)}) %collective-permute-start.3) | collective-permute-done | bytes 49184 | tf_op jit(solution)/shard_map/ppermute | solution.py:362
  61.7 3.0 %collective-permute-done.2.refs_1_ = f32[3,32,128]{2,1,0:T(8,128)S(1)} collective-permute-done((f32[3,32,128]{2,1,0:T(8,128)S(1)}, f32[3,32,128]{2,1,0:T(8,128)S(1)}, u32[]{:S(2)}, u32[]{:S(2)}) %collective-permute-start.2) | collective-permute-done | bytes 49184 | tf_op jit(solution)/shard_map/ppermute | solution.py:362
  64.7 0.0 collective-permute-done.1.refs_0_
  64.7 1.6 %add_earlier.1 = f32[9,32,128]{2,1,0:T(8,128)} custom-call(f32[9,32,128]{2,1,0:T(8,128)} %get-tuple-element.15.base_in, f32[3,32,128]{2,1,0:T(8,128)S(1)} %collective-permute-done.other_ref, f32[3,32,128]{2,1,0:T(8,128)S(1)} %collective-permute-done.1.refs_0_, f32[3,32,128]{2,1,0:T(8,128)S(1)} %collective-permute-done.2.refs_1_, ...), custom_call_target="tpu_custom_call" | custom-call | tf_op jit(solution)/shard_map/add_earlier/pallas_call | solution.py:368
  (10 shorter events, 0.1 us)
Async XLA Ops:
  4.0 25.7 %all-to-all-start = ((f32[32,24,128]{2,1,0:T(8,128)}), f32[32,24,128]{2,1,0:T(8,128)S(1)}, u32[]{:S(2)}, u32[]{:S(2)}) async-start(f32[32,24,128]{2,1,0:T(8,128)} %gather_blocks.1), calls=%async_computation | async-start | bytes 786432 | tf_op jit(solution)/shard_map/all_to_all | solution.py:405
  19.0 10.6 %copy-start = (s32[32]{0:T(128)S(1)}, s32[32]{0:T(128)}, u32[]{:S(2)}) copy-start(s32[32]{0:T(128)} %count_ref.1) | copy-start | bytes 388
  54.0 3.5 %collective-permute-start = (f32[3,32,128]{2,1,0:T(8,128)S(1)}, f32[3,32,128]{2,1,0:T(8,128)S(1)}, u32[]{:S(2)}, u32[]{:S(2)}) collective-permute-start(f32[3,32,128]{2,1,0:T(8,128)S(1)} %get-tuple-element.16), channel_id=1, source_target_pairs={{0,32},{32,0},{64,96},{96,64},{128,160},{160,128},{192,224},{224,1... | collective-permute-start | bytes 147464 | tf_op jit(solution)/shard_map/ppermute | solution.py:362
  57.4 4.3 %collective-permute-start.3 = (f32[3,32,128]{2,1,0:T(8,128)S(1)}, f32[3,32,128]{2,1,0:T(8,128)S(1)}, u32[]{:S(2)}, u32[]{:S(2)}) collective-permute-start(f32[3,32,128]{2,1,0:T(8,128)S(1)} %add.85), channel_id=1, source_target_pairs={{0,192},{32,224},{64,128},{96,160},{128,64},{160,96},{192,0},{224,... | collective-permute-start | bytes 147464 | tf_op jit(solution)/shard_map/ppermute | solution.py:362
  60.3 4.4 %collective-permute-start.2 = (f32[3,32,128]{2,1,0:T(8,128)S(1)}, f32[3,32,128]{2,1,0:T(8,128)S(1)}, u32[]{:S(2)}, u32[]{:S(2)}) collective-permute-start(f32[3,32,128]{2,1,0:T(8,128)S(1)} %add.85), channel_id=1, source_target_pairs={{0,128},{32,160},{64,192},{96,224},{128,0},{160,32},{192,64},{224,... | collective-permute-start | bytes 147464 | tf_op jit(solution)/shard_map/ppermute | solution.py:362
  60.6 4.1 %collective-permute-start.1 = (f32[3,32,128]{2,1,0:T(8,128)S(1)}, f32[3,32,128]{2,1,0:T(8,128)S(1)}, u32[]{:S(2)}, u32[]{:S(2)}) collective-permute-start(f32[3,32,128]{2,1,0:T(8,128)S(1)} %add.85), channel_id=1, source_target_pairs={{0,64},{32,96},{64,0},{96,32},{128,192},{160,224},{192,128},{224,1... | collective-permute-start | bytes 147464 | tf_op jit(solution)/shard_map/ppermute | solution.py:362

commit v4 on v3

--- a/solution.py
+++ b/solution.py
@@ -96,7 +96,7 @@
             jnp.where(top, pltpu.roll(p, (ROWS - 3 * m) % ROWS, 0), pltpu.roll(p, ROWS - 6, 0))[0:8]
             for p in parts
         ]
-        weight_ref[slot, m] = jnp.concatenate(made + [blank], 0).astype(bf16)
+        weight_ref[slot, m] = jnp.concatenate(made + [blank, blank, made[2]], 0).astype(bf16)
 
 
 def target_features(rows, target_ref, t):
@@ -126,7 +126,7 @@
         ],
         0,
     )
-    total = jnp.zeros((64, 2 * LANES), f32)
+    total = jnp.zeros((48, 2 * LANES), f32)
     for j in range(begin, end, 2):
         slots = [[table_ref[t * list_len + q] for q in (j, j + 1)] for t in ids]
         features = jnp.concatenate(
@@ -136,9 +136,10 @@
             ],
             0,
         )
-        weights = jnp.concatenate(
-            [jnp.concatenate([weight_ref[s[0], m], weight_ref[s[1], m]], 1) for s in slots], 0
-        )
+        ones, twos = [
+            jnp.concatenate([weight_ref[s[0], m], weight_ref[s[1], m]], 1) for s in slots
+        ]
+        weights = jnp.concatenate([ones[0:16], twos[0:16], ones[16:32] + twos[32:48]], 0)
         squares = jnp.dot(features, both, preferred_element_type=f32)
         inverse = lax.rsqrt(squares)
         kernel = inverse * inverse * inverse
@@ -148,8 +149,8 @@
         total = total + jnp.dot(weights, low, preferred_element_type=f32)
     sums = []
     for q in range(2):
-        mine = total[32 * q : 32 * q + 32, LANES * q : LANES * q + LANES]
-        sums.append(mine[0:8] + mine[8:16] + mine[16:24])
+        mine = total[:, LANES * q : LANES * q + LANES]
+        sums.append(mine[16 * q : 16 * q + 8] + mine[16 * q + 8 : 16 * q + 16] + mine[32 + 8 * q : 40 + 8 * q])
     return sums
 
 
@@ -432,7 +433,7 @@
 
     kept = (
         ((blocks, LANES, LANES), bf16),
-        ((blocks, 3, 32, LANES), bf16),
+        ((blocks, 3, 48, LANES), bf16),
         ((blocks, 3, LANES, LANES), bf16),
         ((blocks, 3, 8, LANES), f32),
     )
@@ -465,7 +466,7 @@
         out_specs=(hbm(), vmem()),
         scratch_shapes=[
             pltpu.VMEM((slots, LANES, LANES), bf16),
-            pltpu.VMEM((slots, 3, 32, LANES), bf16),
+            pltpu.VMEM((slots, 3, 48, LANES), bf16),
             pltpu.VMEM(*kept[2]),
             pltpu.VMEM(*kept[3]),
             pltpu.VMEM((9, blocks, LANES), f32),

time: 67.3 us -> 66.5 us (0.988); the launches traced: 66.5 us -> 66.6 us
  waiting for transfers between devices: 5.6 us -> 6.82 us
  Pallas kernels: 38.2 us -> 37.1 us
    pallas_call x1, Pallas kernels: 9.67 us -> 8.45 us  [shards(): pl.pallas_call(near_kernel, out_shape=tuple((pltpu.HBM(*k) for k in kept)...]
    all_to_all x1, waiting for transfers between devices: 0.95 us -> 2.18 us  [shards(): far = lax.all_to_all(send, 'space', 0, 0, tiled=True)]
  transfers between devices with their start and end apart: 5 -> 5, of which waited for: 4 -> 4; matrix products, arithmetic and copies ran while one was open for 5% -> 5% of each run, Pallas kernels for 15% -> 13%
where the time goes in v4:
time: 66.5 us; the launch traced here: 66.6 us
  Pallas kernels  37.1 us (56%)
  starting transfers between devices  17.9 us (27%)
  waiting for transfers between devices  6.82 us (10%)
  other arithmetic  2.94 us (4%)
  local copies, waits for them, and re-layouts  1.49 us (2%)
    pallas_call x1, Pallas kernels, shards(): pl.pallas_call(rest_kernel, out_shape=(pltpu.HBM((9, blocks, LANES), f32)...  24.5 us
    all_to_all x1, starting transfers between devices, shards(): far = lax.all_to_all(send, 'space', 0, 0, tiled=True)  11.9 us
    pallas_call x1, Pallas kernels, shards(): pl.pallas_call(near_kernel, out_shape=tuple((pltpu.HBM(*k) for k in kept)...  8.45 us
    ppermute x4, starting transfers between devices, swap(): return lax.ppermute(value, 'tm', [(i, i ^ k) for i in range(slices)])  6.06 us
    ppermute x4, waiting for transfers between devices, swap(): return lax.ppermute(value, 'tm', [(i, i ^ k) for i in range(slices)])  4.65 us
    pallas_call x1, Pallas kernels, shards(): pl.pallas_call(gather_kernel, out_shape=jax.ShapeDtypeStruct((groups, 24,...  2.6 us
    all_to_all x1, waiting for transfers between devices, shards(): far = lax.all_to_all(send, 'space', 0, 0, tiled=True)  2.18 us
    pallas_call x1, Pallas kernels, add_earlier(): pl.pallas_call(functools.partial(sum_kernel, shifts), out_shape=jax.Shape...  1.59 us
  transfers between devices with their start and end apart: 5, of which 4 were waited for; matrix products, arithmetic and copies ran while one was open for 5% of the time, Pallas kernels for 13%

profile of v4, /device:TPU:1, one launch (start us, length us, event | category | flops | bytes accessed | tf_op | source)
XLA Modules:
  0.0 66.6 jit_solution(6306003320295585931)
XLA Ops:
  0.0 0.9 %select_reduce_fusion.3 = (s32[1024]{0:T(1024)S(1)}, s32[1024]{0:T(1024)S(1)}) fusion(s32[1024,12]{0,1:T(8,128)} %param.8, s32[]{:T(128)S(6)} %axis_index.12), kind=kLoop, calls=%fused_computation.10 | loop fusion | flops 292864 | bytes 57348 | tf_op jit(solution)/shard_map/reduce_min | solution.py:391
  0.9 0.1 reduce_min.27
  1.0 0.1 reduce_max.14
  1.1 0.1 reduce_min.28
  1.2 0.1 reduce_max.18
  1.3 2.6 %gather_blocks.1 = f32[32,24,128]{2,1,0:T(8,128)} custom-call(s32[2,32]{1,0:T(2,128)S(1)} %pad_add_fusion.1.pick_ref, f32[9,32,128]{2,1,0:T(8,128)} %bitcast.4, f32[3,4096]{1,0:T(4,128)} %strength_in.3), custom_call_target="tpu_custom_call" | custom-call | tf_op jit(solution)/shard_map/gather_blocks/pallas_call | solution.py:393
  3.9 11.9 %all-to-all-start = ((f32[32,24,128]{2,1,0:T(8,128)}), f32[32,24,128]{2,1,0:T(8,128)S(1)}, u32[]{:S(2)}, u32[]{:S(2)}) async-start(f32[32,24,128]{2,1,0:T(8,128)} %gather_blocks.1), calls=%async_computation | async-start | bytes 786432 | tf_op jit(solution)/shard_map/all_to_all | solution.py:406
  15.8 0.8 %constant_dynamic-slice_fusion = s32[32,12]{0,1:T(8,128)S(1)} fusion(s32[1024,12]{0,1:T(8,128)} %param.8, s32[]{:T(128)S(6)} %select_n.95), kind=kLoop, calls=%fused_computation.51 | loop fusion | bytes 3076 | tf_op jit(solution)/shard_map/dynamic_slice | solution.py:408
  16.6 0.1 copy.12
  16.7 0.1 reshape.163
  16.8 0.1 select_reduce_fusion.5
  16.9 0.1 select_reduce_fusion.4
  17.0 0.1 reduce_sum.66
  17.1 0.1 copy.13
  17.2 0.8 %compare_convert_fusion = (s32[32,12]{0,1:T(8,128)S(1)}, s32[32,12]{0,1:T(8,128)S(1)}) fusion(s32[32,12]{0,1:T(8,128)S(1)} %copy.13, s32[]{:T(128)S(6)} %axis_index.12, s32[1024,12]{0,1:T(8,128)} %param.8, s32[]{:T(128)S(6)} %select_n.95), kind=kLoop, calls=%fused_computation.33 | loop fusion | flops 10752 | bytes 6152 | tf_op jit(solution)/shard_map/convert_element_type | solution.py:416
  18.1 0.2 convert_reduce_fusion
  18.2 0.1 select_reduce_fusion.1
  18.4 0.1 select_reduce_fusion.6
  18.5 0.2 select_reduce_fusion.7
  18.7 0.1 copy.14
  18.8 0.1 reshape.164
  18.9 0.1 pad_add_fusion.table_ref
  19.0 0.0 copy-start
  19.0 8.4 %near_rates.1 = (bf16[32,128,128]{2,1,0:T(8,128)(2,1)}, bf16[32,3,48,128]{3,2,1,0:T(8,128)(2,1)}, bf16[32,3,128,128]{3,2,1,0:T(8,128)(2,1)}, f32[32,3,8,128]{3,2,1,0:T(8,128)}) custom-call(s32[420]{0:T(512)S(1)} %pad_add_fusion.table_ref, f32[9,32,128]{2,1,0:T(8,128)} %bitcast.5, f32[3,4096]{1,0:T(4,128)} %strength_in.3), custom_call_target="tpu_custom_call" | custom-call | flops 10000000000 | bytes 6000000 | tf_op jit(solution)/shard_map/near_rates/pallas_call | solution.py:440
  27.4 2.2 %all-to-all-done.far_ref = f32[32,24,128]{2,1,0:T(8,128)S(1)} async-done(((f32[32,24,128]{2,1,0:T(8,128)}), f32[32,24,128]{2,1,0:T(8,128)S(1)}, u32[]{:S(2)}, u32[]{:S(2)}) %all-to-all-start) | async-done | bytes 393248 | tf_op jit(solution)/shard_map/all_to_all | solution.py:406
  29.6 0.0 copy-done
  29.6 24.5 %rest_rates.1 = (f32[9,32,128]{2,1,0:T(8,128)}, f32[3,32,128]{2,1,0:T(8,128)S(1)}) custom-call(s32[420]{0:T(512)S(1)} %pad_add_fusion.table_ref, s32[32]{0:T(128)S(1)} %copy-done, f32[32,24,128]{2,1,0:T(8,128)S(1)} %all-to-all-done.far_ref, bf16[32,128,128]{2,1,0:T(8,128)(2,1)} %get-tuple-element.11.near_feature, ...), custom_call_target="tpu_custom_call" | custom-call | tf_op jit(solution)/shard_map/rest_rates/pallas_call | solution.py:459
  54.1 2.6 %collective-permute-start = (f32[3,32,128]{2,1,0:T(8,128)S(1)}, f32[3,32,128]{2,1,0:T(8,128)S(1)}, u32[]{:S(2)}, u32[]{:S(2)}) collective-permute-start(f32[3,32,128]{2,1,0:T(8,128)S(1)} %get-tuple-element.16), channel_id=1, source_target_pairs={{0,32},{32,0},{64,96},{96,64},{128,160},{160,128},{192,224},{224,1... | collective-permute-start | bytes 147464 | tf_op jit(solution)/shard_map/ppermute | solution.py:363
  56.6 0.9 %collective-permute-done.other_ref = f32[3,32,128]{2,1,0:T(8,128)S(1)} collective-permute-done((f32[3,32,128]{2,1,0:T(8,128)S(1)}, f32[3,32,128]{2,1,0:T(8,128)S(1)}, u32[]{:S(2)}, u32[]{:S(2)}) %collective-permute-start) | collective-permute-done | bytes 49184 | tf_op jit(solution)/shard_map/ppermute | solution.py:363
  57.5 2.8 %collective-permute-start.3 = (f32[3,32,128]{2,1,0:T(8,128)S(1)}, f32[3,32,128]{2,1,0:T(8,128)S(1)}, u32[]{:S(2)}, u32[]{:S(2)}) collective-permute-start(f32[3,32,128]{2,1,0:T(8,128)S(1)} %add.85), channel_id=1, source_target_pairs={{0,192},{32,224},{64,128},{96,160},{128,64},{160,96},{192,0},{224,... | collective-permute-start | bytes 147464 | tf_op jit(solution)/shard_map/ppermute | solution.py:363
  60.4 0.3 collective-permute-start.2
  60.7 0.3 collective-permute-start.1
  61.0 0.8 %collective-permute-done.3.refs_2_ = f32[3,32,128]{2,1,0:T(8,128)S(1)} collective-permute-done((f32[3,32,128]{2,1,0:T(8,128)S(1)}, f32[3,32,128]{2,1,0:T(8,128)S(1)}, u32[]{:S(2)}, u32[]{:S(2)}) %collective-permute-start.3) | collective-permute-done | bytes 49184 | tf_op jit(solution)/shard_map/ppermute | solution.py:363
  61.8 3.0 %collective-permute-done.2.refs_1_ = f32[3,32,128]{2,1,0:T(8,128)S(1)} collective-permute-done((f32[3,32,128]{2,1,0:T(8,128)S(1)}, f32[3,32,128]{2,1,0:T(8,128)S(1)}, u32[]{:S(2)}, u32[]{:S(2)}) %collective-permute-start.2) | collective-permute-done | bytes 49184 | tf_op jit(solution)/shard_map/ppermute | solution.py:363
  64.8 0.0 collective-permute-done.1.refs_0_
  64.8 1.6 %add_earlier.1 = f32[9,32,128]{2,1,0:T(8,128)} custom-call(f32[9,32,128]{2,1,0:T(8,128)} %get-tuple-element.15.base_in, f32[3,32,128]{2,1,0:T(8,128)S(1)} %collective-permute-done.other_ref, f32[3,32,128]{2,1,0:T(8,128)S(1)} %collective-permute-done.1.refs_0_, f32[3,32,128]{2,1,0:T(8,128)S(1)} %collective-permute-done.2.refs_1_, ...), custom_call_target="tpu_custom_call" | custom-call | tf_op jit(solution)/shard_map/add_earlier/pallas_call | solution.py:369
  (10 shorter events, 0.1 us)
Async XLA Ops:
  3.9 25.7 %all-to-all-start = ((f32[32,24,128]{2,1,0:T(8,128)}), f32[32,24,128]{2,1,0:T(8,128)S(1)}, u32[]{:S(2)}, u32[]{:S(2)}) async-start(f32[32,24,128]{2,1,0:T(8,128)} %gather_blocks.1), calls=%async_computation | async-start | bytes 786432 | tf_op jit(solution)/shard_map/all_to_all | solution.py:406
  19.0 10.6 %copy-start = (s32[32]{0:T(128)S(1)}, s32[32]{0:T(128)}, u32[]{:S(2)}) copy-start(s32[32]{0:T(128)} %count_ref.1) | copy-start | bytes 388
  54.1 3.4 %collective-permute-start = (f32[3,32,128]{2,1,0:T(8,128)S(1)}, f32[3,32,128]{2,1,0:T(8,128)S(1)}, u32[]{:S(2)}, u32[]{:S(2)}) collective-permute-start(f32[3,32,128]{2,1,0:T(8,128)S(1)} %get-tuple-element.16), channel_id=1, source_target_pairs={{0,32},{32,0},{64,96},{96,64},{128,160},{160,128},{192,224},{224,1... | collective-permute-start | bytes 147464 | tf_op jit(solution)/shard_map/ppermute | solution.py:363
  57.5 4.3 %collective-permute-start.3 = (f32[3,32,128]{2,1,0:T(8,128)S(1)}, f32[3,32,128]{2,1,0:T(8,128)S(1)}, u32[]{:S(2)}, u32[]{:S(2)}) collective-permute-start(f32[3,32,128]{2,1,0:T(8,128)S(1)} %add.85), channel_id=1, source_target_pairs={{0,192},{32,224},{64,128},{96,160},{128,64},{160,96},{192,0},{224,... | collective-permute-start | bytes 147464 | tf_op jit(solution)/shard_map/ppermute | solution.py:363
  60.4 4.4 %collective-permute-start.2 = (f32[3,32,128]{2,1,0:T(8,128)S(1)}, f32[3,32,128]{2,1,0:T(8,128)S(1)}, u32[]{:S(2)}, u32[]{:S(2)}) collective-permute-start(f32[3,32,128]{2,1,0:T(8,128)S(1)} %add.85), channel_id=1, source_target_pairs={{0,128},{32,160},{64,192},{96,224},{128,0},{160,32},{192,64},{224,... | collective-permute-start | bytes 147464 | tf_op jit(solution)/shard_map/ppermute | solution.py:363
  60.7 4.1 %collective-permute-start.1 = (f32[3,32,128]{2,1,0:T(8,128)S(1)}, f32[3,32,128]{2,1,0:T(8,128)S(1)}, u32[]{:S(2)}, u32[]{:S(2)}) collective-permute-start(f32[3,32,128]{2,1,0:T(8,128)S(1)} %add.85), channel_id=1, source_target_pairs={{0,64},{32,96},{64,0},{96,32},{128,192},{160,224},{192,128},{224,1... | collective-permute-start | bytes 147464 | tf_op jit(solution)/shard_map/ppermute | solution.py:363
